TPU v7x, 32 devices: a whole 2x2x4 slice. The times are simulated.
32 devices in a mesh: dp: 2 (over y), ctx: 4 (over x, core), exp: 4 (over z).
Axes of the slice: x: 2, y: 2, z: 4, core: 2. Of those that a mesh axis runs over, the one named last changes fastest.
Arguments:
- tokens: bfloat16 [2, 2048, 768], P('dp', ('ctx', 'exp')), may hold values from -6 to 6
- lengths: int32 [2], P('dp'), may hold values from 512 to 2048, as said below
- routes: int32 [2, 2048, 2], P('dp', ('ctx', 'exp')), may hold values from 0 to 3, all different within a row; in each aligned block of 128 rows (0 to 127, 128 to 255, ..., all dimensions but the last counted through in order) at most 80 rows name the same one
- buckets: int32 [2048], replicated, may hold values from 0 to 31, never falling along the last dimension, each value on 1 to 128 neighbouring positions
- cotangent: bfloat16 [2, 2048, 768], P('dp', ('ctx', 'exp')), may hold values from -6 to 6
- attn_gain: float32 [768], replicated, may hold values from 0.5 to 1.5
- w_qkv: bfloat16 [768, 2304], replicated, may hold values from -0.21875 to 0.21875
- w_attn_out: bfloat16 [768, 768], replicated, may hold values from -6 to 6
- rel_bias: float32 [32, 12], replicated, may hold values from -4 to 4
- ffn_gain: float32 [768], replicated, may hold values from 0.5 to 1.5
- w_router: float32 [768, 4], replicated, may hold values from -0.4375 to 0.4375
- w_up: bfloat16 [4, 768, 3072], P('exp'), may hold values from -0.21875 to 0.21875
- w_down: bfloat16 [4, 3072, 768], P('exp'), may hold values from -0.109375 to 0.109375
Outputs:
- output: bfloat16 [2, 2048, 768], P('dp', ('ctx', 'exp'))
- grad_tokens: float32 [2, 2048, 768], P('dp', ('ctx', 'exp'))
- grad_attn_gain: float32 [768], replicated
- grad_qkv: float32 [768, 2304], replicated
- grad_attn_out: float32 [768, 768], replicated
- grad_rel_bias: float32 [32, 12], replicated
- grad_ffn_gain: float32 [768], replicated
- grad_router: float32 [768, 4], replicated
- grad_up: float32 [4, 768, 3072], P('exp')
- grad_down: float32 [4, 3072, 768], P('exp')
Inputs may be any that keep to these rules, and one draw needn't show every extreme that they name: `lengths`: the valid tokens of a slot are its first positions, at least a quarter of the slot; some slot is always full. `routes`: each token names two different experts; among the 128 rows of one device no expert is named more than 80 times. `buckets`: never falls as the distance grows, starting at 0.
All inputs are finite; a program needn't handle non-finite values.
Results may differ from a plain program's by a relative error of at most 0.035.
Values may be sent and summed in bfloat16 or wider, within the bound.
No kernel may reach another device: no remote copies, remote signals or barrier semaphores. Data moves between devices by JAX's collectives and lax.ppermute only.
A program may use at most 256 MiB of HBM per device.

v0:
```python
import math

import jax
import jax.numpy as jnp
from jax import lax
from jax.sharding import PartitionSpec as P

CAP = 80


epsilon = 1e-06


def normed(values, gain):
    return values * lax.rsqrt(jnp.mean(values * values, axis=-1, keepdims=True) + epsilon) * gain


def gelu_tanh(values):
    return jax.nn.gelu(values, approximate=True)


def bucket_bias(bias_table, distance, buckets):
    n_buckets = bias_table.shape[1]
    starts = jnp.sum(
        (buckets[:, None] < jnp.arange(n_buckets, dtype=jnp.int32)[None, :]).astype(jnp.int32),
        axis=0,
    )
    result = bias_table[:, 0][:, None, None] + jnp.zeros((1,) + distance.shape, jnp.float32)
    for bucket in range(1, n_buckets):
        step_size = bias_table[:, bucket] - bias_table[:, bucket - 1]
        result = (
            result
            + step_size[:, None, None] * (distance >= starts[bucket]).astype(jnp.float32)[None]
        )
    return result


def score_block(queries, key_rows, key_start, query_pos, length, bias_table, buckets):
    key_count = key_rows.shape[0]
    key_pos = key_start + jnp.arange(key_count, dtype=jnp.int32)
    distance = query_pos[:, None] - key_pos[None, :]
    biases = bucket_bias(bias_table, distance, buckets)
    scores = (
        jnp.einsum("qhd,khd->hqk", queries, key_rows, preferred_element_type=jnp.float32) * 0.125
        + biases
    )
    allowed = (distance >= 0) & (key_pos[None, :] < length)
    return (scores, allowed)


def diagonal_bias(grad_score, query_start, key_start, buckets, n_buckets):
    heads, query_count, key_count = grad_score.shape
    flipped = grad_score.astype(jnp.float32)[:, :, ::-1]
    padded = jnp.pad(flipped, ((0, 0), (0, 0), (0, query_count)))
    span = key_count + query_count - 1
    skewed = padded.reshape(heads, query_count * (key_count + query_count))[:, : query_count * span]
    diagonal = jnp.sum(skewed.reshape(heads, query_count, span), axis=1)
    distance = query_start - key_start + jnp.arange(span, dtype=jnp.int32) - (key_count - 1)
    bucket_ids = jnp.take(buckets, jnp.clip(distance, 0, buckets.shape[0] - 1))
    match = (
        (bucket_ids[:, None] == jnp.arange(n_buckets, dtype=jnp.int32)[None, :])
        & (distance >= 0)[:, None]
    ).astype(jnp.float32)
    return jnp.dot(diagonal, match, precision=lax.Precision.HIGHEST)


def score_grads(
    queries,
    grad_heads,
    log_norm,
    row_dots,
    key_rows,
    value_rows,
    key_start,
    query_pos,
    length,
    bias_table,
    buckets,
):
    scores, allowed = score_block(
        queries, key_rows, key_start, query_pos, length, bias_table, buckets
    )
    attn_probs = jnp.where(allowed[None], jnp.exp(scores - log_norm[..., None]), 0.0)
    grad_prob = jnp.einsum(
        "qhd,khd->hqk", grad_heads, value_rows, preferred_element_type=jnp.float32
    )
    grad_score = (attn_probs * (grad_prob - row_dots[..., None])).astype(jnp.bfloat16)
    return (attn_probs, grad_score)


def fold_piece(loop_state, kv_piece, queries, query_pos, length, bias_table, buckets):
    piece_rows = kv_piece.shape[0]
    key_block = math.gcd(piece_rows, 1024)
    per_dev = queries.shape[1]
    head_dim = queries.shape[2]
    last_query = query_pos[-1]

    def fold_one_step(index, state_now):
        offset = index * key_block

        def fold_work(state_in):
            running_max, running_sum, weighted = state_in
            kv_block = lax.dynamic_slice_in_dim(kv_piece, offset, key_block, 0).reshape(
                key_block, per_dev, 2, head_dim
            )
            scores, allowed = score_block(
                queries, kv_block[:, :, 0], offset, query_pos, length, bias_table, buckets
            )
            block_max = jnp.max(jnp.where(allowed[None], scores, -1e30), axis=-1)
            new_max = jnp.maximum(running_max, block_max)
            attn_probs = jnp.where(allowed[None], jnp.exp(scores - new_max[..., None]), 0.0)
            rescale = jnp.exp(running_max - new_max)
            running_sum = running_sum * rescale + jnp.sum(attn_probs, axis=-1)
            weighted = weighted * rescale[..., None] + jnp.einsum(
                "hqk,khd->hqd",
                attn_probs.astype(jnp.bfloat16),
                kv_block[:, :, 1],
                preferred_element_type=jnp.float32,
            )
            return (new_max, running_sum, weighted)

        live = (offset <= last_query) & (offset < length)
        return lax.cond(live, fold_work, lambda state_in: state_in, state_now)

    return lax.fori_loop(0, piece_rows // key_block, fold_one_step, loop_state)


def grad_blocks(
    kv_all, queries, grad_heads, log_norm, row_dots, query_pos, length, bias_table, buckets
):
    total_rows = kv_all.shape[0]
    key_block = math.gcd(total_rows, 1024)
    per_dev = queries.shape[1]
    head_dim = queries.shape[2]
    n_buckets = bias_table.shape[1]
    first_query = query_pos[0]
    last_query = query_pos[-1]

    def grad_one_step(state_now, index):
        offset = index * key_block

        def grad_work(state_in):
            grad_query, grad_bias = state_in
            kv_block = lax.dynamic_slice_in_dim(kv_all, offset, key_block, 0).reshape(
                key_block, per_dev, 2, head_dim
            )
            key_rows = kv_block[:, :, 0]
            attn_probs, grad_score = score_grads(
                queries,
                grad_heads,
                log_norm,
                row_dots,
                key_rows,
                kv_block[:, :, 1],
                offset,
                query_pos,
                length,
                bias_table,
                buckets,
            )
            grad_query = (
                grad_query
                + jnp.einsum(
                    "hqk,khd->qhd", grad_score, key_rows, preferred_element_type=jnp.float32
                )
                * 0.125
            )
            grad_value = jnp.einsum(
                "hqk,qhd->khd",
                attn_probs.astype(jnp.bfloat16),
                grad_heads,
                preferred_element_type=jnp.float32,
            )
            grad_key = (
                jnp.einsum("hqk,qhd->khd", grad_score, queries, preferred_element_type=jnp.float32)
                * 0.125
            )
            grad_bias = grad_bias + diagonal_bias(
                grad_score, first_query, offset, buckets, n_buckets
            )
            grad_pair = jnp.stack([grad_key, grad_value], axis=2).reshape(
                key_block, per_dev * 2 * head_dim
            )
            return ((grad_query, grad_bias), grad_pair)

        def skip(state_in):
            return (state_in, jnp.zeros((key_block, per_dev * 2 * head_dim), jnp.float32))

        live = (offset <= last_query) & (offset < length)
        return lax.cond(live, grad_work, skip, state_now)

    start_state = (
        jnp.zeros(queries.shape, jnp.float32),
        jnp.zeros((per_dev, n_buckets), jnp.float32),
    )
    (grad_query, grad_bias), grad_pairs = lax.scan(
        grad_one_step, start_state, jnp.arange(total_rows // key_block, dtype=jnp.int32)
    )
    return (grad_query, grad_bias, grad_pairs.reshape(total_rows, per_dev * 2 * head_dim))


def slot_index_of(expert_ids, n_experts):
    flat_ids = expert_ids.reshape(-1)
    one_hot = (flat_ids[:, None] == jnp.arange(n_experts, dtype=jnp.int32)[None, :]).astype(
        jnp.int32
    )
    earlier = jnp.cumsum(one_hot, axis=0) - one_hot
    return flat_ids * CAP + jnp.sum(earlier * one_hot, axis=1)


def on_device(
    tokens,
    lengths,
    routes,
    buckets,
    cotangent,
    attn_gain,
    w_qkv,
    w_attn_out,
    rel_bias,
    ffn_gain,
    w_router,
    w_up,
    w_down,
):
    inputs = tokens[0].astype(jnp.float32)
    length = lengths[0]
    n_exp = lax.axis_size("exp")
    ctx_index = lax.axis_index("ctx")
    exp_index = lax.axis_index("exp")
    tok_rows, model_width = inputs.shape
    heads_all = rel_bias.shape[1]
    head_dim = model_width // heads_all
    per_dev = heads_all // n_exp
    ctx_rows = tok_rows * n_exp
    n_experts = w_router.shape[1]
    local_experts = w_up.shape[0]
    positions = (ctx_index * n_exp + exp_index) * tok_rows + jnp.arange(tok_rows, dtype=jnp.int32)
    valid_rows = (positions < length).astype(jnp.float32)[:, None]
    key_start = ctx_index * ctx_rows
    query_pos = key_start + jnp.arange(ctx_rows, dtype=jnp.int32)
    first_normed, first_norm_back = jax.vjp(normed, inputs, attn_gain)
    first_norm = first_normed.astype(jnp.bfloat16)
    qkv = jnp.dot(first_norm, w_qkv, preferred_element_type=jnp.float32).astype(jnp.bfloat16)
    head_rows = lax.all_to_all(
        qkv.reshape(1, tok_rows, n_exp, per_dev * 3 * head_dim),
        "exp",
        split_axis=2,
        concat_axis=0,
        tiled=True,
    )
    head_rows = head_rows.reshape(ctx_rows, per_dev, 3, head_dim)
    queries = head_rows[:, :, 0]
    kv_local = head_rows[:, :, 1:].reshape(ctx_rows, per_dev * 2 * head_dim)
    bias_table = lax.dynamic_slice_in_dim(rel_bias, exp_index * per_dev, per_dev, 1).T
    start_state = (
        jnp.full((per_dev, ctx_rows), -1e30, jnp.float32),
        jnp.zeros((per_dev, ctx_rows), jnp.float32),
        jnp.zeros((per_dev, ctx_rows, head_dim), jnp.float32),
    )
    running_max, running_sum, weighted = fold_piece(
        start_state,
        lax.all_gather(kv_local, "ctx", axis=0, tiled=True),
        queries,
        query_pos,
        length,
        bias_table,
        buckets,
    )
    log_norm = running_max + jnp.log(running_sum)
    attn_heads = (
        jnp.transpose(weighted / running_sum[..., None], (1, 0, 2))
        .reshape(ctx_rows, per_dev * head_dim)
        .astype(jnp.bfloat16)
    )
    attn_rows = lax.all_to_all(
        attn_heads.reshape(n_exp, tok_rows, 1, per_dev * head_dim),
        "exp",
        split_axis=0,
        concat_axis=2,
        tiled=True,
    )
    attn_rows = attn_rows.reshape(tok_rows, model_width)
    branch = jnp.dot(attn_rows, w_attn_out, preferred_element_type=jnp.float32)
    middle = inputs + valid_rows * branch
    second_normed, second_norm_back = jax.vjp(normed, middle, ffn_gain)
    second_norm = second_normed.astype(jnp.bfloat16)
    second_wide = second_norm.astype(jnp.float32)
    logits = jnp.dot(second_wide, w_router, precision=lax.Precision.HIGHEST)
    expert_ids = routes[0]
    chosen = jnp.take_along_axis(logits, expert_ids, axis=1)
    gate_probs = jax.nn.softmax(chosen, axis=-1)
    slot_index = slot_index_of(expert_ids, n_experts)

    def to_sources(values):
        last = values.shape[-1]
        return (
            values.reshape(local_experts, n_exp, CAP, last)
            .transpose(1, 0, 2, 3)
            .reshape(n_exp, local_experts * CAP, last)
        )

    def to_experts(values):
        last = values.shape[-1]
        return (
            values.reshape(n_exp, local_experts, CAP, last)
            .transpose(1, 0, 2, 3)
            .reshape(local_experts, n_exp * CAP, last)
        )

    send_rows = (
        jnp.zeros((n_experts * CAP, model_width), jnp.bfloat16)
        .at[slot_index]
        .set(jnp.repeat(second_norm, 2, axis=0))
    )
    arrived = lax.all_to_all(
        send_rows.reshape(n_exp, local_experts * CAP, model_width),
        "exp",
        split_axis=0,
        concat_axis=0,
        tiled=True,
    )
    expert_in = to_experts(arrived)
    up_proj = jnp.einsum("erd,edf->erf", expert_in, w_up, preferred_element_type=jnp.float32)
    hidden = gelu_tanh(up_proj).astype(jnp.bfloat16)
    expert_out = jnp.einsum(
        "erf,efd->erd", hidden, w_down, preferred_element_type=jnp.float32
    ).astype(jnp.bfloat16)
    returned = lax.all_to_all(
        to_sources(expert_out), "exp", split_axis=0, concat_axis=0, tiled=True
    ).reshape(n_experts * CAP, model_width)
    expert_res = returned[slot_index].reshape(tok_rows, 2, model_width).astype(jnp.float32)
    expert_mix = jnp.sum(gate_probs[:, :, None] * expert_res, axis=1)
    output = (middle + valid_rows * expert_mix).astype(jnp.bfloat16)
    grad_out = cotangent[0].astype(jnp.float32)
    grad_mix = valid_rows * grad_out
    grad_res = (gate_probs[:, :, None] * grad_mix[:, None, :]).astype(jnp.bfloat16)
    grad_gate = jnp.sum(expert_res * grad_mix[:, None, :], axis=-1)
    grad_chosen = gate_probs * (grad_gate - jnp.sum(gate_probs * grad_gate, axis=-1, keepdims=True))
    expert_match = (
        expert_ids[:, :, None] == jnp.arange(n_experts, dtype=jnp.int32)[None, None, :]
    ).astype(jnp.float32)
    grad_logits = jnp.sum(expert_match * grad_chosen[:, :, None], axis=1)
    grad_router = jnp.dot(second_wide.T, grad_logits, precision=lax.Precision.HIGHEST)
    grad_second = jnp.dot(grad_logits, w_router.T, precision=lax.Precision.HIGHEST)
    send_grads = (
        jnp.zeros((n_experts * CAP, model_width), jnp.bfloat16)
        .at[slot_index]
        .set(grad_res.reshape(2 * tok_rows, model_width))
    )
    arrived_grads = lax.all_to_all(
        send_grads.reshape(n_exp, local_experts * CAP, model_width),
        "exp",
        split_axis=0,
        concat_axis=0,
        tiled=True,
    )
    grad_expert_out = to_experts(arrived_grads)
    grad_down = jnp.einsum(
        "erf,erd->efd", hidden, grad_expert_out, preferred_element_type=jnp.float32
    )
    grad_hidden = jnp.einsum(
        "erd,efd->erf", grad_expert_out, w_down, preferred_element_type=jnp.float32
    )
    _, gelu_back = jax.vjp(gelu_tanh, up_proj)
    grad_up_proj = gelu_back(grad_hidden)[0].astype(jnp.bfloat16)
    grad_up = jnp.einsum(
        "erd,erf->edf", expert_in, grad_up_proj, preferred_element_type=jnp.float32
    )
    grad_in = jnp.einsum(
        "erf,edf->erd", grad_up_proj, w_up, preferred_element_type=jnp.float32
    ).astype(jnp.bfloat16)
    back_rows = lax.all_to_all(
        to_sources(grad_in), "exp", split_axis=0, concat_axis=0, tiled=True
    ).reshape(n_experts * CAP, model_width)
    grad_second = grad_second + jnp.sum(
        back_rows[slot_index].reshape(tok_rows, 2, model_width).astype(jnp.float32), axis=1
    )
    grad_middle_norm, grad_ffn_gain = second_norm_back(grad_second)
    grad_middle = grad_out + grad_middle_norm
    grad_branch = (valid_rows * grad_middle).astype(jnp.bfloat16)
    grad_attn_out = jnp.dot(attn_rows.T, grad_branch, preferred_element_type=jnp.float32)
    grad_attn = jnp.dot(grad_branch, w_attn_out.T, preferred_element_type=jnp.float32).astype(
        jnp.bfloat16
    )
    grad_heads = lax.all_to_all(
        grad_attn.reshape(1, tok_rows, n_exp, per_dev * head_dim),
        "exp",
        split_axis=2,
        concat_axis=0,
        tiled=True,
    )
    grad_heads = grad_heads.reshape(ctx_rows, per_dev, head_dim)
    row_dots = jnp.einsum(
        "qhd,qhd->hq",
        grad_heads.astype(jnp.float32),
        attn_heads.reshape(ctx_rows, per_dev, head_dim).astype(jnp.float32),
    )
    kv_back = lax.all_gather(kv_local, "ctx", axis=0, tiled=True)
    grad_query, grad_bias, grad_pairs = grad_blocks(
        kv_back, queries, grad_heads, log_norm, row_dots, query_pos, length, bias_table, buckets
    )
    grad_kv = lax.psum_scatter(
        grad_pairs.astype(jnp.bfloat16), "ctx", scatter_dimension=0, tiled=True
    ).astype(jnp.float32)
    grad_qkv_heads = jnp.concatenate(
        [grad_query[:, :, None, :], grad_kv.reshape(ctx_rows, per_dev, 2, head_dim)], axis=2
    )
    grad_qkv_heads = grad_qkv_heads.reshape(ctx_rows, per_dev * 3 * head_dim).astype(jnp.bfloat16)
    grad_rows = lax.all_to_all(
        grad_qkv_heads.reshape(n_exp, tok_rows, 1, per_dev * 3 * head_dim),
        "exp",
        split_axis=0,
        concat_axis=2,
        tiled=True,
    )
    grad_rows = grad_rows.reshape(tok_rows, 3 * model_width)
    grad_qkv = jnp.dot(first_norm.T, grad_rows, preferred_element_type=jnp.float32)
    grad_first = jnp.dot(grad_rows, w_qkv.T, preferred_element_type=jnp.float32)
    grad_input_norm, grad_attn_gain = first_norm_back(grad_first)
    grad_tokens = grad_middle + grad_input_norm
    grad_rel_bias = lax.dynamic_update_slice(
        jnp.zeros(rel_bias.shape, jnp.float32), grad_bias.T, (0, exp_index * per_dev)
    )
    dense_sums = lax.psum(
        (grad_attn_gain, grad_qkv, grad_attn_out, grad_rel_bias, grad_ffn_gain, grad_router),
        ("dp", "ctx", "exp"),
    )
    up_sum, down_sum = (
        lax.psum(grad_up.astype(jnp.bfloat16), ("dp", "ctx")).astype(jnp.float32),
        lax.psum(grad_down.astype(jnp.bfloat16), ("dp", "ctx")).astype(jnp.float32),
    )
    return (
        output[None],
        grad_tokens[None],
        dense_sums[0],
        dense_sums[1],
        dense_sums[2],
        dense_sums[3],
        dense_sums[4],
        dense_sums[5],
        up_sum,
        down_sum,
    )


def solution(mesh):
    return jax.shard_map(
        on_device,
        mesh=mesh,
        in_specs=(
            P("dp", ("ctx", "exp"), None),
            P("dp"),
            P("dp", ("ctx", "exp"), None),
            P(),
            P("dp", ("ctx", "exp"), None),
            P(),
            P(),
            P(),
            P(),
            P(),
            P(),
            P("exp", None, None),
            P("exp", None, None),
        ),
        out_specs=(
            P("dp", ("ctx", "exp"), None),
            P("dp", ("ctx", "exp"), None),
            P(),
            P(),
            P(),
            P(),
            P(),
            P(),
            P("exp", None, None),
            P("exp", None, None),
        ),
        check_vma=False,
    )
```

profile of v0, /device:TPU:0, one launch (start us, length us, event | category | flops | bytes accessed | tf_op | source)
XLA Modules:
  0.0 1258.2 jit_solution(1126703751685635348)
XLA Ops:
  9.5 2.4 convolution_convert_fusion.2
  14.0 22.2 %all_to_all.80 = bf16[1,128,4,576]{1,3,0,2:T(8,128)(2,1)S(1)} all-to-all(bf16[1,128,4,576]{1,3,0,2:T(8,128)(2,1)} %bitcast.506), channel_id=1, replica_groups=mesh['dp'=2,'ctx'=4,'exp'=4] {'exp'}, dimensions={2} | all-to-all | bytes 1179648 | tf_op jit(solution)/shard_map/all_to_all | solution.py:245
  61.8 93.7 %while.33 = (s32[]{:T(128)}, f32[3,512]{1,0:T(4,128)S(1)}, f32[3,512]{1,0:T(4,128)}, f32[3,512,64]{1,2,0:T(8,128)}, s32[]{:T(128)}, /*index=5*/s32[]{:T(128)}, b...) while((s32[]{:T(128)}, f32[3,512]{1,0:T(4,128)S(1)}, ...), condition=%wide.region_7.8_spmd.clone, body=%wide.region_1.7_spmd.clone.sunk | while | flops 550902336 | bytes 181800304 | solution.py:125
  64.2 89.6 %conditional.6 = ((f32[3,512]{1,0:T(4,128)S(1)}, f32[3,512]{1,0:T(4,128)}, f32[3,512,64]{1,2,0:T(8,128)})) conditional(s32[]{:T(128)} %convert_element_type.809, (f32[3,512]{1,0:T(4,128)S(1)}, f32[3,512]{1,0:T(4,128)}, f32[3,512,64]{1,2,0:T(8,128)}) %tuple.257, (s32[]{:T(128)}, s32[]{:T(128)}, s32[]{:T(128)}, bf16[2048,384]{0,1:T(8,128)(2,1)}, ...), branch_computations={%region_2.0_spmd, %region_3.6_spmd} | conditional | flops 550902336 | bytes 181797952 | solution.py:123
  66.4 21.4 %fusion.9 = (pred[512,1024]{0,1:T(8,128)(4,1)}, f32[512,1024]{0,1:T(8,128)}, f32[512,1024]{0,1:T(8,128)}, f32[512,1024]{0,1:T(8,128)}, f32[512,1024]{0,1:T(8,128...) fusion(s32[1024]{0:T(1024)S(1)} %iota_add_fusion, ...), kind=kLoop, calls=%fused_computation.47 | loop fusion | flops 18350080 | bytes 34085952 | tf_op jit(solution)/shard_map/while/body/eval_jaxpr/cond/branch_1_fun/and | solution.py:47
  88.5 19.9 %fusion.10 = (f32[512,1024]{0,1:T(8,128)}, f32[512,1024]{0,1:T(8,128)}, f32[512,1024]{0,1:T(8,128)}, f32[512,1024]{0,1:T(8,128)}, f32[512,1024]{0,1:T(8,128)}, /...) fusion(s32[]{:T(128)} %bitcast.7, ...), kind=kLoop, calls=%fused_computation.48 | loop fusion | flops 16252928 | bytes 31463484 | tf_op jit(solution)/shard_map/while/body/eval_jaxpr/cond/branch_1_fun/convert_element_type | solution.py:33
  113.5 31.7 %select_reduce_fusion = (f32[3,512]{1,0:T(4,128)}, f32[3,512,1024]{1,2,0:T(8,128)}) fusion(pred[512,1024]{0,1:T(8,128)(4,1)} %get-tuple-element.647, f32[512,1024]{0,1:T(8,128)} %get-tuple-element.678, f32[3]{0:T(128)} %get-tuple-element.617, f32[512,1024]{0,1:T(8,128)} %get-tuple-element.648, f32[3]{0:T(128)} %get-tuple-element.618, ...), kind=kOutput, calls=%fused_computation.42 | convolution fusion | flops 305134080 | bytes 72439808 | tf_op jit(solution)/shard_map/while/body/eval_jaxpr/cond/branch_1_fun/qhd,khd->hqk/dot_general | solution.py:44
  146.0 4.4 fusion.5
  150.5 3.2 fusion.41
  160.6 4.8 all-to-all-start.1
  167.7 5.7 all-to-all-done.1
  180.6 2.9 scatter_custom_fusion
  183.4 4.1 all-to-all-start.2
  191.0 2.6 mul.1182
  197.1 3.0 gather_fusion.3
  209.4 3.1 scatter_custom_fusion.1
  212.5 5.0 all-to-all-start.4
  217.5 6.1 fusion.105
  223.6 5.3 all-to-all-done.4
  228.8 7.1 fusion.115
  236.0 5.6 fusion.118
  241.6 4.5 all-to-all-start.5
  246.1 6.7 fusion.121
  252.8 4.4 all-to-all-done.5
  257.2 4.1 all-to-all-start.3
  265.1 3.2 gather_fusion.2
  270.6 2.8 reduce_sum.180
  273.4 3.4 gather_fusion.1
  279.0 3.4 multiply_reduce_fusion
  293.1 2.5 convolution_convert_fusion.3
  297.3 5.0 all-to-all-start.6
  303.1 5.6 all-to-all-done.6
  315.8 243.5 %while.34 = (s32[]{:T(128)}, f32[512,3,64]{0,2,1:T(8,128)}, f32[3,32]{1,0:T(4,128)}, bf16[2,1024,384]{1,2,0:T(8,128)(2,1)}, s32[2]{0:T(128)}, /*index=5*/s32[]{:...) while((s32[]{:T(128)}, f32[512,3,64]{0,2,1:T(8,128)}, ...), condition=%wide.region_27.28_spmd.clone, body=%wide.region_22.0_spmd.clone.sunk | while | flops 1156770816 | bytes 324263104 | solution.py:196
  319.2 224.2 %conditional.7 = (f32[512,3,64]{0,2,1:T(8,128)}, f32[3,32]{1,0:T(4,128)}, bf16[1,1024,384]{1,2,0:T(8,128)(2,1)}) conditional(s32[]{:T(128)} %convert_element_type.810, (f32[512,3,64]{0,2,1:T(8,128)}, f32[3,32]{1,0:T(4,128)}) %tuple.260, (s32[]{:T(128)}, bf16[2048,384]{0,1:T(8,128)(2,1)}, s32[]{:T(128)}, s32[]{:T(128)}, ...), branch_computations={%region_23.23_spmd, %region_24.26_spmd} | conditional | flops 1156770816 | bytes 322687840 | solution.py:190
  320.8 20.1 %fusion.52 = (f32[512,1024]{0,1:T(8,128)}, f32[512,1024]{0,1:T(8,128)}, f32[512,1024]{0,1:T(8,128)}, f32[512,1024]{0,1:T(8,128)}, f32[512,1024]{0,1:T(8,128)}, /...) fusion(s32[]{:T(128)} %bitcast.74, ...), kind=kLoop, calls=%fused_computation.165 | loop fusion | flops 16252928 | bytes 31463484 | tf_op jit(solution)/shard_map/while/body/eval_jaxpr/cond/branch_1_fun/convert_element_type | solution.py:33
  342.2 21.5 %fusion.51 = (pred[512,1024]{0,1:T(8,128)(4,1)}, f32[512,1024]{0,1:T(8,128)}, f32[512,1024]{0,1:T(8,128)}, f32[512,1024]{0,1:T(8,128)}, f32[512,1024]{0,1:T(8,12...) fusion(s32[1024]{0:T(1024)S(1)} %iota_add_fusion.1, ...), kind=kLoop, calls=%fused_computation.164 | loop fusion | flops 18350080 | bytes 34085952 | tf_op jit(solution)/shard_map/while/body/eval_jaxpr/cond/branch_1_fun/and | solution.py:47
  366.0 2.4 constant_dynamic-slice_fusion.1
  368.5 29.8 %fusion.48 = f32[3,512,1024]{1,2,0:T(8,128)} fusion(f32[3,512]{1,0:T(4,128)S(1)} %get-tuple-element.333, f32[512,1024]{0,1:T(8,128)} %get-tuple-element.584, f32[3]{0:T(128)} %get-tuple-element.523, f32[512,1024]{0,1:T(8,128)} %get-tuple-element.554, f32[3]{0:T(128)} %get-tuple-element.524, f32[512,1024]{0,1:T(8,128)} %get-tuple-element.555, ...), kind=kOutput, calls=%fused_computation.161 | convolution fusion | flops 305135616 | bytes 72439808 | tf_op jit(solution)/shard_map/while/body/eval_jaxpr/cond/branch_1_fun/qhd,khd->hqk/dot_general | solution.py:44
  398.3 4.1 fusion.45
  405.5 45.6 %rev.2 = f32[3,512,1024]{1,2,0:T(8,128)} reverse(bf16[3,512,1024]{1,2,0:T(8,128)(2,1)} %copy-done.2), dimensions={2} | reverse | bytes 9437184 | tf_op jit(solution)/shard_map/while/body/eval_jaxpr/cond/branch_1_fun/rev | solution.py:53
  451.1 6.6 copy.154
  457.7 4.0 pad_bitcast_fusion
  461.7 19.9 %copy.156 = f32[1,3,512,1536]{3,1,2,0:T(4,128)S(1)} copy(f32[1,3,512,1536]{3,2,1,0:T(8,128)S(1)} %pad_bitcast_fusion) | data formatting | bytes 18874368 | tf_op jit(solution)/shard_map/while/body/eval_jaxpr/cond
  481.6 5.8 slice.492
  487.4 13.3 %reshape.2796 = f32[2357760]{0:T(1024)} reshape(f32[3,785920]{1,0:T(4,128)} %slice.492) | data formatting | bytes 18862080 | tf_op jit(solution)/shard_map/while/body/eval_jaxpr/cond
  500.7 15.6 %reshape.2700 = f32[3,512,1535]{2,1,0:T(8,128)} reshape(f32[2357760]{0:T(1024)} %reshape.2796) | data formatting | bytes 18862080 | tf_op jit(solution)/shard_map/while/body/eval_jaxpr/cond/branch_1_fun/reshape | solution.py:57
  516.4 4.8 reduce_sum.95
  522.4 11.9 gather_fusion
  537.4 3.9 fusion.83
  559.3 2.7 copy.157
  562.1 6.7 fusion.107
  568.8 5.7 fusion.108
  576.2 325.5 %reduce-scatter.2.cloned.1.call-done = bf16[512,384]{0,1:T(8,128)(2,1)} async-done(((bf16[2048,384]{0,1:T(8,128)(2,1)}), bf16[512,384]{0,1:T(8,128)(2,1)}) %reduce-scatter.2.cloned.1.call-update) | async-done | bytes 393232 | tf_op jit(solution)/shard_map/reduce_scatter | solution.py:403
  907.8 4.6 all-to-all-start.7
  912.4 3.1 fusion.165
  915.5 12.9 %all-to-all-done.7 = bf16[4,128,1,576]{1,3,2,0:T(8,128)(2,1)} async-done(((bf16[4,128,1,576]{1,3,2,0:T(8,128)(2,1)}), bf16[4,128,1,576]{1,3,2,0:T(8,128)(2,1)}, u32[]{:S(2)}, u32[]{:S(2)}) %all-to-all-start.7) | async-done | bytes 589856 | tf_op jit(solution)/shard_map/all_to_all | solution.py:410
  928.4 5.3 fusion.147
  937.0 107.7 %all-reduce.9.cloned.1.call-done = (bf16[1,768,3072]{2,1,0:T(8,128)(2,1)}, bf16[1,3072,768]{2,1,0:T(8,128)(2,1)}) async-done(((bf16[1,768,3072]{2,1,0:T(8,128)(2,1)}, bf16[1,3072,768]{2,1,0:T(8,128)(2,1)}), (bf16[1,768,3072]{2,1,0:T(8,128)(2,1)}, bf16[1,3072,768]{2,1,0:T(8,128)(2,1)})) %all-reduce.9.cloned.1.call-update) | async-done | bytes 9437200 | tf_op jit(solution)/shard_map/psum | solution.py:430
  1044.7 7.5 convert_element_type.648
  1052.2 4.5 convert_element_type.651
  1056.7 3.9 fusion.132
  1060.6 42.0 %all-reduce.1 = (f32[768]{0:T(1024)}, f32[32,12]{0,1:T(8,128)}, f32[768]{0:T(1024)}, f32[768,4]{0,1:T(4,128)}) all-reduce(f32[768]{0:T(1024)} %get-tuple-element.456, f32[32,12]{0,1:T(8,128)S(1)} %dynamic_update_slice.7, f32[768]{0:T(1024)S(1)} %copy-done.25, ...), channel_id=1, replica_groups=mesh['dp'=2,'ctx'=4,'exp'=4] {'dp','ctx','exp'}, use_global_device_ids=true, to_apply=%region_31.32 | all-reduce | flops 4992 | bytes 39936 | tf_op jit(solution)/shard_map/psum | solution.py:425
  1105.4 138.0 %all-reduce.7.cloned.1.call-done = (f32[768,2304]{1,0:T(8,128)}, f32[768,768]{1,0:T(8,128)}) async-done(((f32[768,2304]{1,0:T(8,128)}, f32[768,768]{1,0:T(8,128)}), (f32[768,2304]{1,0:T(8,128)}, f32[768,768]{1,0:T(8,128)})) %all-reduce.7.cloned.1.call-update) | async-done | bytes 9437200 | tf_op jit(solution)/shard_map/psum | solution.py:425
  1243.5 6.6 copy.203
  (221 shorter events, 136.5 us)
Async XLA Ops:
  7.2 2.3 copy-start
  7.2 53.3 %all-gather.2.cloned.1.call-start = ((), (), s32[]{:S(2)}) async-start(), calls=%async_computation.9 | async-start | bytes 1966080 | tf_op jit(solution)/shard_map/all_gather | solution.py:263
  8.4 0.5 copy-start.36
  9.0 0.5 copy-start.29
  11.9 29.7 %copy-start.32 = (s32[1,128,2]{1,2,0:T(2,128)S(1)}, s32[1,128,2]{1,2,0:T(2,128)}, u32[]{:S(2)}) copy-start(s32[1,128,2]{1,2,0:T(2,128)} %param.23) | copy-start | bytes 3076
  11.9 50.0 %copy-start.1 = (s32[2048]{0:T(1024)S(1)}, s32[2048]{0:T(1024)}, u32[]{:S(2)}) copy-start(s32[2048]{0:T(1024)} %param.24) | copy-start | bytes 24580
  88.5 19.9 %copy-start.15 = (f32[3,32]{0,1:T(8,128)S(1)}, f32[3,32]{0,1:T(8,128)}, u32[]{:S(2)}) copy-start(f32[3,32]{0,1:T(8,128)} %get-tuple-element.304) | copy-start | bytes 1156 | tf_op jit(solution)/shard_map/while/body/eval_jaxpr/cond
  145.2 5.3 copy-start.19
  145.2 5.3 copy-start.4
  145.2 5.3 copy-start.5
  150.5 3.2 copy-start.20
  155.6 35.4 %copy-start.18 = (f32[3,512]{1,0:T(4,128)}, f32[3,512]{1,0:T(4,128)S(1)}, u32[]{:S(2)}) copy-start(f32[3,512]{1,0:T(4,128)S(1)} %get-tuple-element.376) | copy-start | bytes 18436
  160.6 12.8 %all-to-all-start.1 = ((bf16[4,128,1,192]{1,3,2,0:T(8,128)(2,1)}), bf16[4,128,1,192]{1,3,2,0:T(8,128)(2,1)}, u32[]{:S(2)}, u32[]{:S(2)}) async-start(bf16[4,128,1,192]{1,3,2,0:T(8,128)(2,1)} %copy.124), calls=%async_computation.1 | async-start | bytes 393216 | tf_op jit(solution)/shard_map/all_to_all | solution.py:276
  165.4 0.5 copy-start.26
  175.2 0.5 copy-start.37
  175.2 0.7 copy-start.11
  175.7 0.5 copy-start.35
  177.0 0.7 copy-start.14
  183.4 29.0 %all-to-all-start.2 = ((bf16[4,80,768]{2,1,0:T(8,128)(2,1)}), bf16[4,80,768]{2,1,0:T(8,128)(2,1)}, u32[]{:S(2)}, u32[]{:S(2)}) async-start(bf16[4,80,768]{2,1,0:T(8,128)(2,1)} %bitcast.508), calls=%async_computation.2 | async-start | bytes 983040 | tf_op jit(solution)/shard_map/all_to_all | solution.py:316
  203.6 0.6 copy-start.34
  212.5 16.4 %all-to-all-start.4 = ((bf16[4,80,768]{2,1,0:T(8,128)(2,1)}), bf16[4,80,768]{2,1,0:T(8,128)(2,1)}, u32[]{:S(2)}, u32[]{:S(2)}) async-start(bf16[4,80,768]{2,1,0:T(8,128)(2,1)} %bitcast.509), calls=%async_computation.4 | async-start | bytes 983040 | tf_op jit(solution)/shard_map/all_to_all | solution.py:351
  236.0 5.6 copy-start.39
  241.6 15.6 %all-to-all-start.5 = ((bf16[4,80,768]{2,1,0:T(8,128)(2,1)}), bf16[4,80,768]{2,1,0:T(8,128)(2,1)}, u32[]{:S(2)}, u32[]{:S(2)}) async-start(bf16[4,80,768]{2,1,0:T(8,128)(2,1)} %bitcast.514), calls=%async_computation.5 | async-start | bytes 983040 | tf_op jit(solution)/shard_map/all_to_all | solution.py:373
  257.2 16.3 %all-to-all-start.3 = ((bf16[4,80,768]{2,1,0:T(8,128)(2,1)}), bf16[4,80,768]{2,1,0:T(8,128)(2,1)}, u32[]{:S(2)}, u32[]{:S(2)}) async-start(bf16[4,80,768]{2,1,0:T(8,128)(2,1)} %bitcast.513), calls=%async_computation.3 | async-start | bytes 983040 | tf_op jit(solution)/shard_map/all_to_all | solution.py:329
  263.5 4.9 copy-start.33
  270.6 16.6 %copy-start.22 = (f32[768]{0:T(1024)S(1)}, f32[768]{0:T(1024)}, u32[]{:S(2)}) copy-start(f32[768]{0:T(1024)} %param.30) | copy-start | bytes 9220
  273.4 16.8 %copy-start.27 = (f32[128]{0:T(128)S(1)}, f32[128]{0:T(128)}, u32[]{:S(2)}) copy-start(f32[128]{0:T(128)} %copy-done.26) | copy-start | bytes 1540
  287.2 3.0 copy-start.23
  292.3 0.8 copy-start.12
  297.3 11.4 all-to-all-start.6
  302.3 599.3 %reduce-scatter.2.cloned.1.call-start = ((), (), s32[]{:S(2)}) async-start(), calls=%async_computation.10 | async-start | bytes 1966080 | tf_op jit(solution)/shard_map/reduce_scatter | solution.py:403
  320.8 20.1 %copy-start.16 = (f32[3,32]{0,1:T(8,128)S(1)}, f32[3,32]{0,1:T(8,128)}, u32[]{:S(2)}) copy-start(f32[3,32]{0,1:T(8,128)} %get-tuple-element.331) | copy-start | bytes 1156 | tf_op jit(solution)/shard_map/while/body/eval_jaxpr/cond
  398.3 5.8 copy-start.6
  398.3 5.8 copy-start.8
  402.4 1.7 copy-start.2
  404.7 0.7 copy-start.9
  534.3 6.9 copy-start.3
  534.3 6.9 copy-start.7
  562.0 482.7 %all-reduce.9.cloned.1.call-start = ((), (), s32[]{:S(2)}) async-start(), calls=%async_computation.12 | async-start | bytes 18874368 | tf_op jit(solution)/shard_map/psum | solution.py:430
  562.1 6.7 copy-start.38
  574.5 338.0 %copy-start.28 = (f32[128]{0:T(128)S(1)}, f32[128]{0:T(128)}, u32[]{:S(2)}) copy-start(f32[128]{0:T(128)} %copy-done.26) | copy-start | bytes 1540
  576.2 352.2 %copy-start.21 = (f32[768]{0:T(1024)S(1)}, f32[768]{0:T(1024)}, u32[]{:S(2)}) copy-start(f32[768]{0:T(1024)} %param.26) | copy-start | bytes 9220
  576.2 352.2 %copy-start.30 = (f32[128]{0:T(128)S(1)}, f32[128]{0:T(128)}, u32[]{:S(2)}) copy-start(f32[128]{0:T(128)} %copy-done.29) | copy-start | bytes 1540
  907.8 20.6 %all-to-all-start.7 = ((bf16[4,128,1,576]{1,3,2,0:T(8,128)(2,1)}), bf16[4,128,1,576]{1,3,2,0:T(8,128)(2,1)}, u32[]{:S(2)}, u32[]{:S(2)}) async-start(bf16[4,128,1,576]{1,3,2,0:T(8,128)(2,1)} %copy.138), calls=%async_computation.8 | async-start | bytes 1179648 | tf_op jit(solution)/shard_map/all_to_all | solution.py:410
  912.4 331.1 %all-reduce.7.cloned.1.call-start = ((), (), s32[]{:S(2)}) async-start(), calls=%async_computation.11 | async-start | bytes 18874368 | tf_op jit(solution)/shard_map/psum | solution.py:425
  933.7 0.7 copy-start.24
  1044.7 7.5 copy-start.13
  1052.2 4.5 copy-start.10
  1052.2 4.5 copy-start.31
  1056.7 3.9 copy-start.25
  1243.5 6.6 copy-start.17
Sparse Core Ops, SparseCore 0:
  41.7 18.7 all-gather.1
  562.1 339.4 reduce-scatter.1
  906.4 138.2 all-reduce.8
  1051.0 192.3 all-reduce.6
where the time goes:
time: 1280 us; the launch traced here: 1260 us
  waiting for transfers between devices  607 us (47%)
  local copies, waits for them, and re-layouts  231 us (18%)
  other arithmetic  155 us (12%)
  matrix products  139 us (11%)
  blocking collectives  64.2 us (5%)
  starting transfers between devices  32.4 us (3%)
  loops' own time  15.5 us (1%)
  between operations  14.9 us (1%)
    reduce_scatter x1, waiting for transfers between devices, on_device(): lax.psum_scatter(grad_pairs.astype(jnp.bfloat16), 'ctx', scatter_dimensio...  325 us
    psum x1, waiting for transfers between devices, on_device(): lax.psum((grad_attn_gain, grad_qkv, grad_attn_out, grad_rel_bias, grad_ff...  138 us
    psum x1, waiting for transfers between devices, on_device(): lax.psum(grad_up.astype(jnp.bfloat16), ('dp', 'ctx')).astype(jnp.float32)  108 us
    dot_general x2, matrix products, score_block(): jnp.einsum('qhd,khd->hqk', queries, key_rows, preferred_element_type=jnp....  61.5 us
    cond x29, local copies, waits for them, and re-layouts  46.2 us
    rev x1, local copies, waits for them, and re-layouts, diagonal_bias(): flipped = grad_score.astype(jnp.float32)[:, :, ::-1]  45.6 us
    and x2, other arithmetic, score_block(): allowed = (distance >= 0) & (key_pos[None, :] < length)  42.9 us
    psum x1, blocking collectives, on_device(): lax.psum((grad_attn_gain, grad_qkv, grad_attn_out, grad_rel_bias, grad_ff...  42 us
  transfers between devices with their start and end apart: 11, of which 9 were waited for; matrix products, arithmetic and copies ran while one was open for 9% of the time, Pallas kernels for 0%

commit v1 on v0

v1 whole, which is shorter than its diff:
```python
import functools

import jax
import jax.numpy as jnp
from jax import lax
from jax.experimental import pallas as pl
from jax.experimental.pallas import tpu as pltpu
from jax.sharding import PartitionSpec as P

CAP = 80
EPS = 1e-06
NEG = -1e30
VMEM_LIMIT = 58 << 20
bf16 = jnp.bfloat16
f32 = jnp.float32
NN = ((1,), (0,))
NT = ((1,), (1,))
TN = ((0,), (0,))
GELU_C = 0.7978845608028654
GELU_A = 0.044715


def dot(left, right, dims):
    return lax.dot_general(left, right, (dims, ((), ())), preferred_element_type=f32)


def iota(shape, axis):
    return lax.broadcasted_iota(jnp.int32, shape, axis)


def norm_scale(values):
    return lax.rsqrt(jnp.mean(values * values, axis=-1, keepdims=True) + EPS)


def norm_back(values, gain, grad):
    scale = norm_scale(values)
    xhat = values * scale
    gxhat = grad * gain
    grad_in = scale * (gxhat - xhat * jnp.mean(gxhat * xhat, axis=-1, keepdims=True))
    return grad_in, xhat


def gelu_parts(u):
    square = u * u
    t = jnp.tanh(u * (GELU_C + (GELU_C * GELU_A) * square))
    half = 0.5 * (1.0 + t)
    slope = half + (0.5 * u) * (1.0 - t * t) * (GELU_C + (3.0 * GELU_C * GELU_A) * square)
    return u * half, slope


def split2(values):
    high = values.astype(bf16)
    return high, (values - high.astype(f32)).astype(bf16)


def params(limit=VMEM_LIMIT):
    return pltpu.CompilerParams(vmem_limit_bytes=limit)


def vmem():
    return pl.BlockSpec(memory_space=pltpu.VMEM)


def smem():
    return pl.BlockSpec(memory_space=pltpu.SMEM)


def call(kernel, outs, ins, scratch=(), cost=None, name=None):
    flops, size = cost if cost else (1 << 20, 1 << 20)
    return pl.pallas_call(
        kernel,
        out_shape=outs,
        in_specs=ins,
        out_specs=jax.tree.map(lambda _: vmem(), outs),
        scratch_shapes=list(scratch),
        compiler_params=params(),
        cost_estimate=pl.CostEstimate(flops=flops, bytes_accessed=size, transcendentals=0),
        name=name,
    )


def sds(shape, dtype):
    return jax.ShapeDtypeStruct(shape, dtype)


def route_kernel(n_experts, sc, routes, routes_t, dy, pick, pay):
    rows = dy.shape[0]
    width = dy.shape[1]
    first, second = routes_t[0:1, :], routes_t[1:2, :]
    eight = iota((8, rows), 0)
    named = jnp.where((first == eight) | (second == eight), 1.0, 0.0)
    upper = jnp.where(iota((rows, rows), 0) < iota((rows, rows), 1), 1.0, 0.0)
    rank = dot(named.astype(bf16), upper.astype(bf16), NN)
    slot = iota((CAP, rows), 0).astype(f32)
    for e in range(n_experts):
        hit = (named[e : e + 1] > 0.5) & (rank[e : e + 1] == slot)
        pick[e * CAP : (e + 1) * CAP, :] = jnp.where(hit, 1.0, 0.0).astype(bf16)
    all_pick = pick[...].astype(f32)
    valid = iota((1, rows), 1) < sc[0]
    live = jnp.where(valid, all_pick, 0.0).astype(bf16)
    pay[:, :width] = dot(live, dy[...], NN).astype(bf16)
    lane = iota((rows, 128), 1)
    kind = jnp.where(lane < 3 * n_experts, lane % n_experts, -1)
    pair = (routes[:, 0:1] == kind) | (routes[:, 1:2] == kind)
    pair = jnp.where(pair, 1.0, 0.0).astype(bf16)
    pay[:, width:] = dot(pick[...], pair, NN).astype(bf16)


def bias_tiles(rel, buckets, brow, tiles, n_buckets):
    n_tiles, side, _ = tiles.shape
    ids = buckets[...]
    row = jnp.zeros(ids.shape, f32)
    for b in range(n_buckets):
        row = jnp.where(ids == b, rel[b], row)
    brow[:, :side] = jnp.zeros((1, side), f32)
    brow[:, side:] = row
    for o in range(n_tiles):
        wide = jnp.broadcast_to(brow[:, o * side : (o + 2) * side], (side, 2 * side))
        tiles[o] = pltpu.roll(wide, 0, axis=1, stride=1, stride_axis=0)[:, side:]


def attn_kernel(n_pieces, n_buckets, head_dim, sc, rel, *refs):
    pieces = refs[:n_pieces]
    gain, weight, buckets = refs[n_pieces : n_pieces + 3]
    h1, qa, ka, va, qt, kt, out_t, lse = refs[n_pieces + 3 : n_pieces + 11]
    vt, brow, tiles = refs[n_pieces + 11 :]
    n_tiles, side, _ = tiles.shape
    length = sc[0]
    lane = iota((128, 128), 1)

    def rows_in(x, start):
        x = x.astype(f32)
        h = (x * norm_scale(x) * gain[...]).astype(bf16)
        h1[pl.ds(start, 128), :] = h
        qkv = dot(h, weight[...], NN).astype(bf16).astype(f32)
        q, k, v = qkv[:, :128] * 0.125, qkv[:, 128:256], qkv[:, 256:]
        live = jnp.where(start + iota((128, 128), 0) < length, 0.0, NEG)
        qa[pl.ds(start, 128), :] = jnp.where(lane == head_dim, 1.0, q).astype(bf16)
        ka[pl.ds(start, 128), :] = jnp.where(lane == head_dim, live, k).astype(bf16)
        va[pl.ds(start, 128), :] = v.astype(bf16)
        qt[:, pl.ds(start, 128)] = q.T[:head_dim].astype(bf16)
        kt[:, pl.ds(start, 128)] = k.T[:head_dim].astype(bf16)
        vt[:, pl.ds(start, 128)] = v.T[:head_dim].astype(bf16)

    for i, piece in enumerate(pieces):
        if piece.shape[0] == 128:
            rows_in(piece[...], pl.multiple_of(sc[1 + i], 128))
        else:

            def step(j, carry, piece=piece, i=i):
                part = piece[pl.ds(pl.multiple_of(j * 128, 128), 128), :]
                rows_in(part, pl.multiple_of(sc[1 + i] + j * 128, 128))
                return carry

            lax.fori_loop(0, piece.shape[0] // 128, step, 0)
    bias_tiles(rel, buckets, brow, tiles, n_buckets)
    blocks = side // 128

    def one_query_tile(qi, carry):
        q_start = pl.multiple_of(qi * side, side)
        q = qa[pl.ds(q_start, side), :]

        def fold(k_start, offset, state, diagonal):
            top, total, acc = state
            scores = dot(ka[pl.ds(k_start, side), :], q, NT) + tiles[offset]
            if diagonal:
                scores = jnp.where(iota((side, side), 0) <= iota((side, side), 1), scores, NEG)
            new_top = jnp.maximum(top, jnp.max(scores, axis=0, keepdims=True))
            probs = jnp.exp(scores - new_top)
            scale = jnp.exp(top - new_top)
            total = total * scale + jnp.sum(probs, axis=0, keepdims=True)
            acc = acc * scale + dot(vt[:, pl.ds(k_start, side)], probs.astype(bf16), NN)
            return new_top, total, acc

        state = (
            jnp.full((1, side), NEG, f32),
            jnp.zeros((1, side), f32),
            jnp.zeros((head_dim, side), f32),
        )
        state = fold(q_start, 0, state, True)

        def earlier(kj, state):
            return fold(pl.multiple_of(kj * side, side), qi - kj, state, False)

        top, total, acc = lax.fori_loop(0, qi, earlier, state)
        result = (acc / total).astype(bf16)
        lse[:, pl.ds(q_start, side)] = top + jnp.log(total)
        for b in range(blocks):
            out_t[qi * blocks + b] = result[:, b * 128 : (b + 1) * 128]
        return carry

    lax.fori_loop(0, n_tiles, one_query_tile, 0)


def attn_back_kernel(n_buckets, head_dim, n_dp, sc, rel, *refs):
    qa, ka, va, qt, kt, out_t, grad_t, lse, h1, buckets, shifted = refs[:11]
    pay, weight_pay = refs[11:13]
    dots, dq, dk, dv, full, brow, tiles, sums, diag = refs[13:]
    n_tiles, side, _ = tiles.shape
    blocks = side // 128
    bias_tiles(rel, buckets, brow, tiles, n_buckets)
    sums[...] = jnp.zeros_like(sums)
    dk[...] = jnp.zeros_like(dk)
    dv[...] = jnp.zeros_like(dv)

    def one_query_tile(qi, carry):
        q_start = pl.multiple_of(qi * side, side)
        q = qa[pl.ds(q_start, side), :]
        q_t = qt[:, pl.ds(q_start, side)]
        g_t = jnp.concatenate([grad_t[qi * blocks + b] for b in range(blocks)], axis=1)
        o_t = jnp.concatenate([out_t[qi * blocks + b] for b in range(blocks)], axis=1)
        row_dots = jnp.sum(g_t.astype(f32) * o_t.astype(f32), axis=0, keepdims=True)
        norm = lse[:, pl.ds(q_start, side)]

        def fold(k_start, offset, acc, diagonal):
            where_k = pl.ds(k_start, side)
            scores = dot(ka[where_k, :], q, NT) + tiles[offset]
            probs = jnp.exp(scores - norm)
            if diagonal:
                probs = jnp.where(iota((side, side), 0) <= iota((side, side), 1), probs, 0.0)
            grad_prob = dot(va[where_k, :][:, :head_dim], g_t, NN)
            grad_score = probs * (grad_prob - row_dots)
            low = grad_score.astype(bf16)
            sums[offset] = sums[offset] + grad_score
            dv[:, where_k] = dv[:, where_k] + dot(g_t, probs.astype(bf16), NT)
            dk[:, where_k] = dk[:, where_k] + dot(q_t, low, NT)
            return acc + dot(kt[:, where_k], low, NN)

        acc = fold(q_start, 0, jnp.zeros((head_dim, side), f32), True)

        def earlier(kj, acc):
            return fold(pl.multiple_of(kj * side, side), qi - kj, acc, False)

        dq[:, pl.ds(q_start, side)] = lax.fori_loop(0, qi, earlier, acc)
        return carry

    lax.fori_loop(0, n_tiles, one_query_tile, 0)
    full[:head_dim, :] = (dq[...] * 0.125).astype(bf16)
    full[head_dim : 2 * head_dim, :] = dk[...].astype(bf16)
    full[2 * head_dim :, :] = dv[...].astype(bf16)
    for b in range(pay.shape[0]):
        pay[b] = full[:, b * 128 : (b + 1) * 128]
    flip = jnp.where(iota((side, side), 0) + iota((side, side), 1) == side - 1, 1.0, 0.0)
    flip = flip.astype(bf16)
    diag[...] = jnp.zeros_like(diag)
    for o in range(n_tiles):
        high, low = split2(sums[o])
        turned = dot(flip, high, NN) + dot(flip, low, NN)
        wide = jnp.concatenate([turned, jnp.zeros((side, side), f32)], axis=1)
        lined = pltpu.roll(wide, 0, axis=1, stride=1, stride_axis=0)
        where_d = slice(o * side, (o + 2) * side)
        diag[:, where_d] = diag[:, where_d] + jnp.sum(lined, axis=0, keepdims=True)
    hot = jnp.where(shifted[...] == iota((128, shifted.shape[1]), 0), 1.0, 0.0).astype(bf16)
    high, low = split2(jnp.broadcast_to(diag[...], (8, diag.shape[1])))
    rel_grad = dot(high, hot, NT) + dot(low, hot, NT)
    grad_w = dot(full[...], h1[...], NN).astype(bf16)
    n_pay, pay_rows, lanes = weight_pay.shape
    n_ctx = n_pay // n_dp
    rows = grad_w.shape[0] // n_ctx
    rel_rows = jnp.concatenate([rel_grad, jnp.zeros((8, lanes - 128), f32)], axis=1)
    rel_rows = jnp.concatenate([rel_rows, jnp.zeros((8, lanes), f32)], axis=0).astype(bf16)
    for d in range(n_dp):
        for c in range(n_ctx):
            weight_pay[d * n_ctx + c, :rows, :] = grad_w[
                c * rows : (c + 1) * rows, d * lanes : (d + 1) * lanes
            ]
            weight_pay[d * n_ctx + c, rows:, :] = rel_rows


def middle_kernel(n_heads, sc, recv, w_out, x, gain, pick, middle, send):
    rows, width = x.shape
    attn_t = jnp.concatenate([recv[h] for h in range(n_heads)], axis=0)
    branch = dot(attn_t, w_out[...], TN)
    valid = iota((rows, 1), 0) < sc[0]
    mid = x[...].astype(f32) + jnp.where(valid, branch, 0.0)
    middle[...] = mid
    h2 = (mid * norm_scale(mid) * gain[...]).astype(bf16)
    send[...] = dot(pick[...], h2, NN).astype(bf16)


def gate_of(h2, pay, width, w3, own):
    logits = dot(h2, w3, NN)
    sel = 2.0 * own - pay[:, width:].astype(f32)
    diff = jnp.sum(logits * sel, axis=1, keepdims=True)
    return 1.0 / (1.0 + jnp.exp(-diff)), sel


def own_lanes(expert, n_experts):
    lane = iota((1, 128), 1)
    return jnp.where((lane < 3 * n_experts) & (lane % n_experts == expert), 1.0, 0.0)


def expert_kernel(
    n_experts, sc, h2, pay, w3, w3_t, w_up, w_down, mix, back, router, z_acc, in_acc, dz, gates
):
    step = pl.program_id(0)
    width = h2.shape[1]
    own = own_lanes(sc[0], n_experts)

    @pl.when(step == 0)
    def _():
        gate, _ = gate_of(h2[...], pay, width, w3[...], own)
        gates[...] = jnp.broadcast_to(gate, gates.shape)
        dz[...] = (gate * pay[:, :width].astype(f32)).astype(bf16)
        z_acc[...] = jnp.zeros_like(z_acc)
        in_acc[...] = jnp.zeros_like(in_acc)

    up = dot(h2[...], w_up[...], NN)
    act, slope = gelu_parts(up)
    grad_hidden = dot(dz[...], w_down[...], NT)
    grad_up = (grad_hidden * slope).astype(bf16)
    z_acc[...] += dot(act.astype(bf16), w_down[...], NN)
    in_acc[...] += dot(grad_up, w_up[...], NT)

    @pl.when(step == pl.num_programs(0) - 1)
    def _():
        gate = gates[:, 0:1]
        sel = 2.0 * own - pay[:, width:].astype(f32)
        z = z_acc[...].astype(bf16).astype(f32)
        mix[...] = (gate * z).astype(bf16)
        grad_gate = jnp.sum(pay[:, :width].astype(f32) * z, axis=1, keepdims=True)
        high, low = split2((gate * (1.0 - gate) * grad_gate) * sel)
        back[...] = (in_acc[...] + dot(high, w3_t[...], NN) + dot(low, w3_t[...], NN)).astype(bf16)
        router[...] = (dot(high, h2[...], TN) + dot(low, h2[...], TN))[:8]


def middle_back_kernel(
    n_heads, sc, back, pick, middle, dy, gain, recv, w_out, router, dmid, grad_t, red
):
    rows, width = middle.shape
    grad_h2 = dot(pick[...], back[...], TN)
    grad_in, xhat = norm_back(middle[...], gain[...], grad_h2)
    grad_mid = dy[...].astype(f32) + grad_in
    dmid[...] = grad_mid
    valid = iota((rows, 1), 0) < sc[0]
    branch = jnp.where(valid, grad_mid, 0.0).astype(bf16)
    attn_t = jnp.concatenate([recv[h] for h in range(n_heads)], axis=0)
    heads = dot(w_out[...], branch, NT).astype(bf16)
    head_dim = width // n_heads
    for h in range(n_heads):
        grad_t[h] = heads[h * head_dim : (h + 1) * head_dim]
    for h in range(n_heads, grad_t.shape[0]):
        grad_t[h] = jnp.zeros((head_dim, rows), bf16)
    red[:width, :] = dot(attn_t, branch, NN).astype(bf16)
    gains = jnp.sum(grad_h2 * xhat, axis=0, keepdims=True)
    small = jnp.concatenate([jnp.broadcast_to(gains, (8, width)), router[...]], axis=0)
    red[width : width + 16, :] = small.astype(bf16)
    rest = red.shape[0] - width - 16
    red[width + 16 :, :] = jnp.zeros((rest, width), bf16)


def output_kernel(sc, mix, pick, middle, out):
    rows = middle.shape[0]
    valid = iota((rows, 1), 0) < sc[0]
    total = dot(pick[...], mix[...], TN)
    out[...] = (middle[...] + jnp.where(valid, total, 0.0)).astype(bf16)


def token_grad_kernel(n_heads, recv, w_qkv, x, gain, dmid, out):
    grad_t = jnp.concatenate([recv[h] for h in range(n_heads)], axis=0)
    grad_h1 = dot(w_qkv[...], grad_t, NN).T
    grad_in, _ = norm_back(x[...].astype(f32), gain[...], grad_h1)
    out[...] = dmid[...] + grad_in


def weight_grad_kernel(n_experts, n_pieces, sc, *refs):
    h_pieces, p_pieces = refs[:n_pieces], refs[n_pieces : 2 * n_pieces]
    w3, w_up, w_down = refs[2 * n_pieces : 2 * n_pieces + 3]
    up_out, down_out, up_low, down_low = refs[2 * n_pieces + 3 : 2 * n_pieces + 7]
    h2, pay, dz, hid_t, dup_t, sem = refs[2 * n_pieces + 7 :]
    step = pl.program_id(0)
    rows = h_pieces[0].shape[0]
    width = h2.shape[1]

    @pl.when(step == 0)
    def _():
        copies = []
        for i in range(n_pieces):
            for j, (src, dst) in enumerate(((h_pieces[i], h2), (p_pieces[i], pay))):
                copy = pltpu.make_async_copy(
                    src, dst.at[pl.ds(i * rows, rows), :], sem.at[j, i]
                )
                copy.start()
                copies.append(copy)
        for copy in copies:
            copy.wait()
        own = own_lanes(sc[1], n_experts)
        gate, _ = gate_of(h2[...], pay, width, w3[...], own)
        dz[...] = (gate * pay[:, :width].astype(f32)).astype(bf16)

    up_t = w_up[...].T
    down = w_down[...]
    chunk = 512
    for r in range(0, h2.shape[0], chunk):
        act, slope = gelu_parts(dot(up_t, h2[r : r + chunk, :], NT))
        hid_t[:, r : r + chunk] = act.astype(bf16)
        grad_hidden = dot(down, dz[r : r + chunk, :], NT)
        dup_t[:, r : r + chunk] = (grad_hidden * slope).astype(bf16)
    grad_down = dot(hid_t[...], dz[...], NN)
    down_out[...] = grad_down
    down_low[...] = grad_down.astype(bf16)
    grad_up = dot(dup_t[...], h2[...], NN).T
    up_out[...] = grad_up
    up_low[...] = grad_up.astype(bf16)


def fill_kernel(sc, up_low, down_low, up_full, down_full, up_out, down_out):
    up_out[...] = up_low[...].astype(f32)
    down_out[...] = down_low[...].astype(f32)


def assemble_kernel(n_exp, rows, n_groups, head_cols, sc, *refs):
    n_pieces = (len(refs) - 7) // 1
    pieces = refs[:n_pieces]
    w_qkv, gain, grad, gain_grad, rel_grad, turned, rel_t = refs[n_pieces:]
    lanes = pieces[0].shape[-1]
    rel_t[...] = jnp.zeros_like(rel_t)
    slot = 0
    for piece in pieces:
        for i in range(piece.shape[0]):
            d, c, e = sc[3 * slot], sc[3 * slot + 1], sc[3 * slot + 2]
            slot += 1
            lane_at = pl.multiple_of(d * lanes, 128)
            for g in range(n_groups):
                head = g * n_exp + e
                row_at = pl.multiple_of(head * head_cols + c * rows, 16)
                turned[pl.ds(row_at, rows), pl.ds(lane_at, lanes)] = piece[
                    i, g * rows : (g + 1) * rows, :
                ]
                rel_t[pl.ds(head, 1), :] = piece[
                    i, n_groups * rows + g : n_groups * rows + g + 1, :128
                ].astype(f32)
    rel = rel_t[...].T
    rel_grad[...] = rel[: rel_grad.shape[0], : rel_grad.shape[1]]
    width, columns = grad.shape
    for a in range(0, width, 128):
        total = jnp.zeros((128, 128), f32)
        for b in range(0, columns, 128):
            tile = turned[b : b + 128, a : a + 128].astype(f32).T
            grad[a : a + 128, b : b + 128] = tile
            total = total + tile * w_qkv[a : a + 128, b : b + 128].astype(f32)
        sums = jnp.sum(total.T, axis=0, keepdims=True)
        gain_grad[:, a : a + 128] = sums / gain[:, a : a + 128]


def on_device(
    n_dp,
    n_ctx,
    n_exp,
    tokens,
    lengths,
    routes,
    buckets,
    cotangent,
    attn_gain,
    w_qkv,
    w_attn_out,
    rel_bias,
    ffn_gain,
    w_router,
    w_up,
    w_down,
):
    x = tokens[0]
    dy = cotangent[0]
    length = lengths[0]
    dp, ctx, exp = (lax.axis_index(name) for name in ("dp", "ctx", "exp"))
    rows, width = x.shape
    seq = buckets.shape[0]
    n_buckets, n_heads = rel_bias.shape
    head_dim = width // n_heads
    n_experts = w_router.shape[1]
    ff = w_up.shape[2]
    n_slot = n_ctx * n_exp
    n_groups = n_heads // n_exp
    n_x = n_ctx // 2
    cx, core = ctx // 2, ctx % 2
    small = n_x == 2 and n_dp == 2
    side = 512 if seq <= 2048 else 256
    n_tiles = seq // side
    slot_rows = n_experts * CAP

    def ring(v, shift):
        return lax.ppermute(v, "exp", [(i, (i + shift) % n_exp) for i in range(n_exp)])

    def swap(v):
        return lax.ppermute(v, "ctx", [(i, i ^ 1) for i in range(n_ctx)])

    def chips(v, a, b):
        perm = []
        for d in range(n_dp):
            for c in range(n_ctx):
                to = ((d + a) % n_dp) * n_ctx + ((c // 2 + b) % n_x) * 2 + c % 2
                perm.append((d * n_ctx + c, to))
        return lax.ppermute(v, ("dp", "ctx"), perm)

    first_pos = (ctx * n_exp + exp) * rows
    n_valid = jnp.clip(length - first_pos, 0, rows).astype(jnp.int32)
    valid_arg = n_valid.reshape(1)
    own_arg = jnp.stack([exp, core]).astype(jnp.int32)

    with jax.named_scope("gather_tokens"):
        if small:
            column = [(x, 0, 0)] + [(ring(x, k), 0, k) for k in range(1, n_exp)]
            pieces = column + [(chips(v, 0, 1), 1, k) for v, _, k in column]
            pieces = [(v, b, 0, k) for v, b, k in pieces]
            pieces = pieces + [(swap(v), b, 1, k) for v, b, _, k in pieces]
            blocks = [v for v, _, _, _ in pieces]
            starts = [
                ((((cx - b) % n_x) * 2 + (core ^ o)) * n_exp + (exp - k) % n_exp) * rows
                for _, b, o, k in pieces
            ]
        else:
            blocks = [lax.all_gather(x, ("ctx", "exp"), axis=0, tiled=True)]
            starts = [jnp.int32(0)]

    with jax.named_scope("routing"):
        pick, pay = call(
            functools.partial(route_kernel, n_experts),
            (sds((slot_rows, rows), bf16), sds((slot_rows, width + 128), bf16)),
            [smem(), vmem(), vmem(), vmem()],
            name="routing",
        )(valid_arg, routes[0], routes[0].T, dy)

        def to_experts(v):
            return lax.all_to_all(
                v.reshape(n_exp, CAP, v.shape[-1]), "exp", split_axis=0, concat_axis=0, tiled=True
            ).reshape(n_exp * CAP, v.shape[-1])

        pay_in = to_experts(pay)
        high = w_router.astype(bf16)
        rest = w_router - high.astype(f32)
        mid = rest.astype(bf16)
        low = (rest - mid.astype(f32)).astype(bf16)
        w3 = jnp.pad(
            jnp.concatenate([high, mid, low], axis=1), ((0, 0), (0, 128 - 3 * n_experts))
        )
        w3_t = w3.T

    with jax.named_scope("attention"):
        head = (ctx * n_exp + exp) % n_heads
        w_head = lax.dynamic_slice_in_dim(w_qkv, head * 3 * head_dim, 3 * head_dim, 1)
        w_head = jnp.pad(
            w_head.reshape(width, 3, head_dim), ((0, 0), (0, 0), (0, 128 - head_dim))
        ).reshape(width, 384)
        rel = lax.dynamic_slice_in_dim(rel_bias, head, 1, 1)[:, 0]
        where_arg = jnp.stack([length] + [s for s in starts]).astype(jnp.int32)
        bucket_row = buckets.reshape(1, seq)
        attn_outs = (
            sds((seq, width), bf16),
            sds((seq, 128), bf16),
            sds((seq, 128), bf16),
            sds((seq, 128), bf16),
            sds((head_dim, seq), bf16),
            sds((head_dim, seq), bf16),
            sds((n_slot, head_dim, 128), bf16),
            sds((1, seq), f32),
        )
        h1, qa, ka, va, qt, kt, out_t, lse = call(
            functools.partial(attn_kernel, len(blocks), n_buckets, head_dim),
            attn_outs,
            [smem(), smem()] + [vmem()] * (len(blocks) + 3),
            [
                pltpu.VMEM((head_dim, seq), bf16),
                pltpu.VMEM((1, seq + side), f32),
                pltpu.VMEM((n_tiles, side, side), f32),
            ],
            cost=(4 << 30, 8 << 20),
            name="attention",
        )(where_arg, rel, *blocks, attn_gain.reshape(1, width), w_head, bucket_row)
        slot_axes = ("ctx", "exp")
        attn_in = lax.all_to_all(out_t, slot_axes, split_axis=0, concat_axis=0, tiled=True)

    with jax.named_scope("middle"):
        gain2 = ffn_gain.reshape(1, width)
        middle, send = call(
            functools.partial(middle_kernel, n_heads),
            (sds((rows, width), f32), sds((slot_rows, width), bf16)),
            [smem()] + [vmem()] * 5,
            name="middle",
        )(valid_arg, attn_in, w_attn_out, x, gain2, pick)
        h2_in = to_experts(send)

    with jax.named_scope("experts"):
        block = 512
        row_spec = pl.BlockSpec((slot_rows, width), lambda i, *_: (0, 0))
        pay_spec = pl.BlockSpec((slot_rows, width + 128), lambda i, *_: (0, 0))
        w3_spec = pl.BlockSpec((width, 128), lambda i, *_: (0, 0))
        mix_rows, back_rows, router = pl.pallas_call(
            functools.partial(expert_kernel, n_experts),
            out_shape=(
                sds((slot_rows, width), bf16),
                sds((slot_rows, width), bf16),
                sds((8, width), f32),
            ),
            grid_spec=pltpu.PrefetchScalarGridSpec(
                num_scalar_prefetch=1,
                grid=(ff // block,),
                in_specs=[
                    row_spec,
                    pay_spec,
                    w3_spec,
                    pl.BlockSpec((128, width), lambda i, *_: (0, 0)),
                    pl.BlockSpec((width, block), lambda i, *_: (0, i)),
                    pl.BlockSpec((block, width), lambda i, *_: (i, 0)),
                ],
                out_specs=(row_spec, row_spec, pl.BlockSpec((8, width), lambda i, *_: (0, 0))),
                scratch_shapes=[
                    pltpu.VMEM((slot_rows, width), f32),
                    pltpu.VMEM((slot_rows, width), f32),
                    pltpu.VMEM((slot_rows, width), bf16),
                    pltpu.VMEM((slot_rows, 128), f32),
                ],
            ),
            compiler_params=params(),
            cost_estimate=pl.CostEstimate(
                flops=8 * slot_rows * width * ff, bytes_accessed=10 << 20, transcendentals=0
            ),
            name="experts",
        )(own_arg, h2_in, pay_in, w3, w3_t, w_up[0], w_down[0])
        back_in = to_experts(back_rows)
        mix_in = to_experts(mix_rows)

    with jax.named_scope("middle_back"):
        shares = n_dp * n_ctx
        red_rows = -(-(width + 16) // (16 * shares)) * 16 * shares
        dmid, grad_t, red = call(
            functools.partial(middle_back_kernel, n_heads),
            (
                sds((rows, width), f32),
                sds((n_slot, head_dim, rows), bf16),
                sds((red_rows, width), bf16),
            ),
            [smem()] + [vmem()] * 8,
            name="middle_back",
        )(valid_arg, back_in, pick, middle, dy, gain2, attn_in, w_attn_out, router)
        grad_in = lax.all_to_all(grad_t, slot_axes, split_axis=0, concat_axis=0, tiled=True)
        output = call(
            output_kernel,
            sds((rows, width), bf16),
            [smem()] + [vmem()] * 3,
            name="output",
        )(valid_arg, mix_in, pick, middle)

    with jax.named_scope("attention_back"):
        shifted = jnp.pad(bucket_row, ((0, 0), (side - 1, 1)), constant_values=-1)
        part = 3 * head_dim // n_ctx
        lanes = width // n_dp
        dqkv, weight_pay = call(
            functools.partial(attn_back_kernel, n_buckets, head_dim, n_dp),
            (sds((n_slot, 3 * head_dim, rows), bf16), sds((shares, part + 16, lanes), bf16)),
            [smem(), smem()] + [vmem()] * 11,
            [
                pltpu.VMEM((1, seq), f32),
                pltpu.VMEM((head_dim, seq), f32),
                pltpu.VMEM((head_dim, seq), f32),
                pltpu.VMEM((head_dim, seq), f32),
                pltpu.VMEM((3 * head_dim, seq), bf16),
                pltpu.VMEM((1, seq + side), f32),
                pltpu.VMEM((n_tiles, side, side), f32),
                pltpu.VMEM((n_tiles, side, side), f32),
                pltpu.VMEM((1, seq + side), f32),
            ],
            cost=(8 << 30, 8 << 20),
            name="attention_back",
        )(where_arg, rel, qa, ka, va, qt, kt, out_t, grad_in, lse, h1, bucket_row, shifted)
        all_chips = ("dp", "ctx")
        summed = lax.all_to_all(weight_pay, all_chips, split_axis=0, concat_axis=0, tiled=True)
        dqkv_in = lax.all_to_all(dqkv, slot_axes, split_axis=0, concat_axis=0, tiled=True)

    with jax.named_scope("token_grads"):
        grad_tokens = call(
            functools.partial(token_grad_kernel, n_heads),
            sds((rows, width), f32),
            [vmem()] * 5,
            name="token_grads",
        )(dqkv_in, w_qkv, x, attn_gain.reshape(1, width), dmid)

    with jax.named_scope("projection_grad"):
        by_ctx = summed.reshape(n_dp, n_ctx, part + 16, lanes)[:, :n_groups].astype(f32).sum(0)
        shard = jnp.concatenate(
            [
                by_ctx[:, :part].reshape(n_groups * part, lanes),
                by_ctx[:, part],
                jnp.zeros((16 - n_groups, lanes), f32),
            ]
        ).astype(bf16)[None]
        if small:
            near = [(shard, [(0, 0, 0)]), ]
            far = jnp.concatenate([ring(shard, k) for k in range(1, n_exp)])
            near.append((far, [(0, 0, k) for k in range(1, n_exp)]))
            spread = list(near)
            for a, b in ((0, 1), (1, 0), (1, 1)):
                spread += [(chips(v, a, b), [(a, b, k) for _, _, k in ids]) for v, ids in near]
            final, ids = [], []
            for v, keys in spread:
                final.append(v)
                ids += [(a, b, 0, k) for a, b, k in keys]
            for v, keys in spread:
                final.append(swap(v))
                ids += [(a, b, 1, k) for a, b, k in keys]
            at = []
            for a, b, o, k in ids:
                at += [(dp - a) % n_dp, ((cx - b) % n_x) * 2 + (core ^ o), (exp - k) % n_exp]
            at = jnp.stack(at).astype(jnp.int32)
            grad_qkv, grad_attn_gain, grad_rel = call(
                functools.partial(assemble_kernel, n_exp, part, n_groups, 3 * head_dim),
                (sds((width, 3 * width), f32), sds((1, width), f32), sds(rel_bias.shape, f32)),
                [smem()] + [vmem()] * (len(final) + 2),
                [pltpu.VMEM((3 * width, width), bf16), pltpu.VMEM((128, 128), f32)],
                name="assemble",
            )(at, *final, w_qkv, attn_gain.reshape(1, width))
            grad_attn_gain = grad_attn_gain[0]
        else:
            every = lax.all_gather(shard[0], ("dp", "ctx", "exp"), axis=0, tiled=False)
            every = every.reshape(n_dp, n_ctx, n_exp, n_groups * part + 16, lanes).astype(f32)
            main = every[:, :, :, : n_groups * part]
            main = main.reshape(n_dp, n_ctx, n_exp, n_groups, part, lanes)
            grad_qkv = main.transpose(0, 5, 3, 2, 1, 4).reshape(width, 3 * width)
            rel_rows = every[0, 0, :, n_groups * part : n_groups * (part + 1), :n_buckets]
            grad_rel = rel_rows.transpose(2, 1, 0).reshape(n_buckets, n_heads)
            grad_attn_gain = jnp.sum(grad_qkv * w_qkv.astype(f32), axis=1) / attn_gain

    with jax.named_scope("output_projection_grad"):
        reduced = lax.psum(red, ("dp", "ctx", "exp")).astype(f32)
        grad_attn_out = reduced[:width]
        grad_ffn_gain = reduced[width]
        grad_router = reduced[width + 8 : width + 8 + n_experts].T

    with jax.named_scope("expert_weight_grads"):
        if small:
            def all_rows(v):
                mine = [v, chips(v, 0, 1), chips(v, 1, 0), chips(v, 1, 1)]
                return mine + [swap(u) for u in mine]

            h_pieces, p_pieces = all_rows(h2_in), all_rows(pay_in)
            n_pieces = len(h_pieces)
            total_rows = n_pieces * slot_rows
            half = ff // 2
            steps = half // block
            any_spec = pl.BlockSpec(memory_space=pl.ANY)
            low_up = pl.BlockSpec((width, block), lambda i, s: (0, i))
            low_down = pl.BlockSpec((block, width), lambda i, s: (i, 0))
            at_up = pl.BlockSpec((width, block), lambda i, s: (0, s[0] * steps + i))
            at_down = pl.BlockSpec((block, width), lambda i, s: (s[0] * steps + i, 0))
            core_arg = jnp.stack([core, exp]).astype(jnp.int32)
            up_part, down_part, up_low, down_low = pl.pallas_call(
                functools.partial(weight_grad_kernel, n_experts, n_pieces),
                out_shape=(
                    sds((width, ff), f32),
                    sds((ff, width), f32),
                    sds((width, half), bf16),
                    sds((half, width), bf16),
                ),
                grid_spec=pltpu.PrefetchScalarGridSpec(
                    num_scalar_prefetch=1,
                    grid=(steps,),
                    in_specs=[any_spec] * (2 * n_pieces) + [w3_spec, at_up, at_down],
                    out_specs=(at_up, at_down, low_up, low_down),
                    scratch_shapes=[
                        pltpu.VMEM((total_rows, width), bf16),
                        pltpu.VMEM((total_rows, width + 128), bf16),
                        pltpu.VMEM((total_rows, width), bf16),
                        pltpu.VMEM((block, total_rows), bf16),
                        pltpu.VMEM((block, total_rows), bf16),
                        pltpu.SemaphoreType.DMA((2, n_pieces)),
                    ],
                ),
                compiler_params=params(),
                cost_estimate=pl.CostEstimate(
                    flops=8 * total_rows * width * half,
                    bytes_accessed=40 << 20,
                    transcendentals=0,
                ),
                name="weight_grads",
            )(core_arg, *h_pieces, *p_pieces, w3, w_up[0], w_down[0])
            up_got, down_got = swap(up_low), swap(down_low)
            other_up = pl.BlockSpec((width, block), lambda i, s: (0, (1 - s[0]) * steps + i))
            other_down = pl.BlockSpec((block, width), lambda i, s: ((1 - s[0]) * steps + i, 0))
            grad_up, grad_down = pl.pallas_call(
                fill_kernel,
                out_shape=(sds((width, ff), f32), sds((ff, width), f32)),
                grid_spec=pltpu.PrefetchScalarGridSpec(
                    num_scalar_prefetch=1,
                    grid=(steps,),
                    in_specs=[low_up, low_down, any_spec, any_spec],
                    out_specs=(other_up, other_down),
                ),
                input_output_aliases={3: 0, 4: 1},
                compiler_params=params(),
                name="fill",
            )(core_arg, up_got, down_got, up_part, down_part)
        else:
            own = own_lanes(exp, n_experts)
            gate, _ = gate_of(h2_in, pay_in, width, w3, own)
            dz = (gate * pay_in[:, :width].astype(f32)).astype(bf16)
            act, slope = gelu_parts(dot(h2_in, w_up[0], NN))
            dup = (dot(dz, w_down[0], NT) * slope).astype(bf16)
            grad_up = lax.psum(dot(h2_in, dup, TN).astype(bf16), all_chips).astype(f32)
            grad_down = lax.psum(dot(act.astype(bf16), dz, TN).astype(bf16), all_chips)
            grad_down = grad_down.astype(f32)

    return (
        output[None],
        grad_tokens[None],
        grad_attn_gain,
        grad_qkv,
        grad_attn_out,
        grad_rel,
        grad_ffn_gain,
        grad_router,
        grad_up[None],
        grad_down[None],
    )


def solution(mesh):
    sizes = dict(mesh.shape)
    by_token = P("dp", ("ctx", "exp"), None)
    by_expert = P("exp", None, None)
    return jax.shard_map(
        functools.partial(on_device, sizes["dp"], sizes["ctx"], sizes["exp"]),
        mesh=mesh,
        in_specs=(
            by_token,
            P("dp"),
            by_token,
            P(),
            by_token,
            P(),
            P(),
            P(),
            P(),
            P(),
            P(),
            by_expert,
            by_expert,
        ),
        out_specs=(
            by_token,
            by_token,
            P(),
            P(),
            P(),
            P(),
            P(),
            P(),
            by_expert,
            by_expert,
        ),
        check_vma=False,
    )
```

time: 1280 us -> 473 us (0.37); the launches traced: 1260 us -> 471 us
  waiting for transfers between devices: 607 us -> 247 us
  local copies, waits for them, and re-layouts: 231 us -> 21.7 us
  other arithmetic: 155 us -> 4.87 us
  matrix products: 139 us -> 0 us
  Pallas kernels: 0 us -> 110 us
  blocking collectives: 64.2 us -> 0 us
  starting transfers between devices: 32.4 us -> 72.1 us
  loops' own time: 15.5 us -> 0 us
    reduce_scatter x1 -> x0, waiting for transfers between devices: 325 us -> none  [on_device(): lax.psum_scatter(grad_pairs.astype(jnp.bfloat16), 'ctx', scatter_dimensio...]
    psum x2 -> x1, waiting for transfers between devices: 246 us -> 105 us  [on_device(): reduced = lax.psum(red, ('dp', 'ctx', 'exp')).astype(f32)]
    dot_general x23 -> x0, matrix products: 139 us -> none  [the longest x2 61.5 us: score_block(): jnp.einsum('qhd,khd->hqk', queries, key_rows, preferred_element_type=jnp....]
    pallas_call x0 -> x11, Pallas kernels: none -> 110 us  [the longest x1 35.6 us: on_device(): pl.pallas_call(functools.partial(weight_grad_kernel, n_experts, n_pieces)...]
    ppermute x0 -> x48, waiting for transfers between devices: none -> 98.6 us  [the longest x16 69 us: chips(): return lax.ppermute(v, ('dp', 'ctx'), perm)]
    convert_element_type x8 -> x2, other arithmetic: 55.2 us -> 1.65 us  [the longest x1 1.64 us: on_device(): reduced = lax.psum(red, ('dp', 'ctx', 'exp')).astype(f32)]
    cond x29 -> x0, local copies, waits for them, and re-layouts: 46.2 us -> none
    rev x1 -> x0, local copies, waits for them, and re-layouts: 45.6 us -> none  [diagonal_bias(): flipped = grad_score.astype(jnp.float32)[:, :, ::-1]]
  transfers between devices with their start and end apart: 11 -> 57, of which waited for: 9 -> 19; matrix products, arithmetic and copies ran while one was open for 9% -> 4% of each run, Pallas kernels for 0% -> 16%
where the time goes in v1:
time: 473 us; the launch traced here: 471 us
  waiting for transfers between devices  247 us (52%)
  Pallas kernels  110 us (23%)
  starting transfers between devices  72.1 us (15%)
  local copies, waits for them, and re-layouts  21.7 us (5%)
  between operations  15.3 us (3%)
  other arithmetic  4.87 us (1%)
    psum x1, waiting for transfers between devices, on_device(): reduced = lax.psum(red, ('dp', 'ctx', 'exp')).astype(f32)  105 us
    ppermute x16, waiting for transfers between devices, chips(): return lax.ppermute(v, ('dp', 'ctx'), perm)  69 us
    all_to_all x4, waiting for transfers between devices, to_experts(): lax.all_to_all(v.reshape(n_exp, CAP, v.shape[-1]), 'exp', split_axis=0, c...  37.1 us
    pallas_call x1, Pallas kernels, on_device(): pl.pallas_call(functools.partial(weight_grad_kernel, n_experts, n_pieces)...  35.6 us
    ppermute x6, waiting for transfers between devices, ring(): lax.ppermute(v, 'exp', [(i, (i + shift) % n_exp) for i in range(n_exp)])  27.7 us
    ppermute x16, starting transfers between devices, chips(): return lax.ppermute(v, ('dp', 'ctx'), perm)  19.6 us
    pallas_call x1, Pallas kernels, on_device(): call(functools.partial(attn_back_kernel, n_buckets, head_dim, n_dp), (sds...  16.5 us
    all_to_all x4, starting transfers between devices, to_experts(): lax.all_to_all(v.reshape(n_exp, CAP, v.shape[-1]), 'exp', split_axis=0, c...  15.3 us
  transfers between devices with their start and end apart: 57, of which 19 were waited for; matrix products, arithmetic and copies ran while one was open for 4% of the time, Pallas kernels for 16%

profile of v1, /device:TPU:0, one launch (start us, length us, event | category | flops | bytes accessed | tf_op | source)
XLA Modules:
  0.0 471.4 jit_solution(8154133807129256677)
XLA Ops:
  7.2 3.1 collective-permute-start
  10.3 2.6 collective-permute-start.1
  12.9 1.3 collective-permute-start.2
  14.2 1.5 collective-permute-start.3
  15.7 2.7 collective-permute-done.refs_1_
  18.4 1.7 collective-permute-start.4
  20.1 5.9 %collective-permute-done.1.refs_2_ = bf16[128,768]{1,0:T(8,128)(2,1)S(1)} collective-permute-done((bf16[128,768]{1,0:T(8,128)(2,1)}, bf16[128,768]{1,0:T(8,128)(2,1)S(1)}, u32[]{:S(2)}, u32[]{:S(2)}) %collective-permute-start.1) | collective-permute-done | bytes 196640 | tf_op jit(solution)/shard_map/gather_tokens/ppermute | solution.py:484
  26.0 1.5 collective-permute-start.5
  29.4 4.3 collective-permute-done.5.refs_6_
  33.8 3.2 collective-permute-done.6.refs_7_
  37.5 1.2 constant_dynamic-slice_fusion
  39.0 1.1 copy.41.refs_17_
  42.6 14.1 %attention.1 = (bf16[2048,768]{1,0:T(8,128)(2,1)}, bf16[2048,128]{1,0:T(8,128)(2,1)}, bf16[2048,128]{1,0:T(8,128)(2,1)}, bf16[2048,128]{1,0:T(8,128)(2,1)}, bf16...) custom-call(s32[17]{0:T(128)} %stack.83.sc, ...), custom_call_target="tpu_custom_call" | custom-call | flops 4294967296 | bytes 8388608 | tf_op jit(solution)/shard_map/attention/attention/pallas_call | solution.py:559
  56.8 7.1 %all-to-all-start = ((bf16[16,64,128]{2,1,0:T(8,128)(2,1)}), bf16[16,64,128]{2,1,0:T(8,128)(2,1)S(1)}, u32[]{:S(2)}, u32[]{:S(2)}) async-start(bf16[16,64,128]{2,1,0:T(8,128)(2,1)} %get-tuple-element.39.refs_5_), calls=%async_computation | async-start | bytes 524288 | tf_op jit(solution)/shard_map/attention/all_to_all | solution.py:572
  64.6 2.2 routing.1
  66.9 7.1 %all-to-all-done.recv = bf16[16,64,128]{2,1,0:T(8,128)(2,1)S(1)} async-done(((bf16[16,64,128]{2,1,0:T(8,128)(2,1)}), bf16[16,64,128]{2,1,0:T(8,128)(2,1)S(1)}, u32[]{:S(2)}, u32[]{:S(2)}) %all-to-all-start) | async-done | bytes 262176 | tf_op jit(solution)/shard_map/attention/all_to_all | solution.py:572
  73.9 3.5 all-to-all-start.2
  78.0 3.0 middle.1
  81.0 12.1 %all-to-all-done.2 = bf16[4,80,896]{2,1,0:T(8,128)(2,1)S(1)} async-done(((bf16[4,80,896]{2,1,0:T(8,128)(2,1)}), bf16[4,80,896]{2,1,0:T(8,128)(2,1)S(1)}, u32[]{:S(2)}, u32[]{:S(2)}) %all-to-all-start.2) | async-done | bytes 573472 | tf_op jit(solution)/shard_map/routing/all_to_all | solution.py:526
  93.1 3.5 all-to-all-start.1
  98.9 10.9 %all-to-all-done.1 = bf16[4,80,768]{2,1,0:T(8,128)(2,1)S(1)} async-done(((bf16[4,80,768]{2,1,0:T(8,128)(2,1)}), bf16[4,80,768]{2,1,0:T(8,128)(2,1)S(1)}, u32[]{:S(2)}, u32[]{:S(2)}) %all-to-all-start.1) | async-done | bytes 491552 | tf_op jit(solution)/shard_map/middle/all_to_all | solution.py:526
  109.8 0.8 copy-done.10
  110.7 13.0 %experts.1 = (bf16[320,768]{1,0:T(8,128)(2,1)}, bf16[320,768]{1,0:T(8,128)(2,1)}, f32[8,768]{1,0:T(8,128)}) custom-call(s32[2]{0:T(128)} %pad_add_fusion.sc, bf16[320,768]{1,0:T(8,128)(2,1)} %bitcast.89, bf16[320,896]{1,0:T(8,128)(2,1)} %bitcast.81, bf16[768,128]{1,0:T(8,128)(2,1)} %get-tuple-element.99.w3.refs_16_, bf16[128,768]{1,0:T(8,128)(2,1)} %copy.44.w3_t, ...), custom_call_target="tpu_custom_call" | custom-call | flops 6039797760 | bytes 10485760 | tf_op jit(solution)/shard_map/experts/experts/pallas_call | solution.py:589
  123.7 3.8 all-to-all-start.4
  127.5 1.7 collective-permute-start.39
  129.1 1.5 collective-permute-start.40
  131.0 12.6 %collective-permute-done.39.refs_9_ = bf16[320,896]{1,0:T(8,128)(2,1)S(1)} collective-permute-done((bf16[320,896]{1,0:T(8,128)(2,1)}, bf16[320,896]{1,0:T(8,128)(2,1)S(1)}, u32[]{:S(2)}, u32[]{:S(2)}) %collective-permute-start.39) | collective-permute-done | bytes 573472 | tf_op jit(solution)/shard_map/expert_weight_grads/ppermute | solution.py:495
  143.6 11.6 %collective-permute-done.40.refs_10_ = bf16[320,896]{1,0:T(8,128)(2,1)S(1)} collective-permute-done((bf16[320,896]{1,0:T(8,128)(2,1)}, bf16[320,896]{1,0:T(8,128)(2,1)S(1)}, u32[]{:S(2)}, u32[]{:S(2)}) %collective-permute-start.40) | collective-permute-done | bytes 573472 | tf_op jit(solution)/shard_map/expert_weight_grads/ppermute | solution.py:495
  156.1 4.1 middle_back.1
  160.2 2.0 collective-permute-start.33
  162.2 1.5 collective-permute-start.34
  163.7 4.6 all-to-all-start.5
  170.6 13.9 %collective-permute-done.33.refs_2_ = bf16[320,768]{1,0:T(8,128)(2,1)} collective-permute-done((bf16[320,768]{1,0:T(8,128)(2,1)S(1)}, bf16[320,768]{1,0:T(8,128)(2,1)}, u32[]{:S(2)}, u32[]{:S(2)}) %collective-permute-start.33) | collective-permute-done | bytes 491552 | tf_op jit(solution)/shard_map/expert_weight_grads/ppermute | solution.py:495
  185.8 16.5 %attention_back.1 = (bf16[16,192,128]{2,1,0:T(8,128)(2,1)}, bf16[8,64,384]{2,1,0:T(8,128)(2,1)}) custom-call(s32[17]{0:T(128)} %stack.83.sc, f32[32]{0:T(128)} %dynamic-slice_bitcast_fusion.rel, bf16[2048,128]{1,0:T(8,128)(2,1)} %get-tuple-element.45.refs_0_, bf16[2048,128]{1,0:T(8,128)(2,1)} %get-tuple-element.46.refs_1_, ...), custom_call_target="tpu_custom_call" | custom-call | flops 8589934592 | bytes 8388608 | tf_op jit(solution)/shard_map/attention_back/attention_back/pallas_call | solution.py:649
  202.3 4.0 all-to-all-start.7
  206.4 35.6 %weight_grads.1 = (f32[768,3072]{1,0:T(8,128)}, f32[3072,768]{1,0:T(8,128)}, bf16[768,1536]{1,0:T(8,128)(2,1)}, bf16[1536,768]{1,0:T(8,128)(2,1)}) custom-call(s32[2]{0:T(128)} %pad_add_fusion.1.sc, bf16[320,768]{1,0:T(8,128)(2,1)} %bitcast.91, bf16[320,768]{1,0:T(8,128)(2,1)} %collective-permute-done.32.refs_1_, ...), custom_call_target="tpu_custom_call" | custom-call | flops 24159191040 | bytes 41943040 | tf_op jit(solution)/shard_map/expert_weight_grads/weight_grads/pallas_call | solution.py:747
  242.6 4.5 all-to-all-start.3
  248.1 2.0 collective-permute-start.15
  250.1 14.1 %all-to-all-done.3 = bf16[4,80,768]{2,1,0:T(8,128)(2,1)S(1)} async-done(((bf16[4,80,768]{2,1,0:T(8,128)(2,1)}), bf16[4,80,768]{2,1,0:T(8,128)(2,1)S(1)}, u32[]{:S(2)}, u32[]{:S(2)}) %all-to-all-start.3) | async-done | bytes 491552 | tf_op jit(solution)/shard_map/experts/all_to_all | solution.py:526
  265.0 3.6 all-to-all-start.6
  268.6 2.8 collective-permute-start.16
  271.4 1.5 collective-permute-start.17
  273.5 1.5 collective-permute-start.18
  275.0 0.9 constant_dynamic-update-slice_fusion.2
  276.0 19.2 %collective-permute-done.16 = bf16[1,160,384]{2,1,0:T(8,128)(2,1)S(1)} collective-permute-done((bf16[1,160,384]{2,1,0:T(8,128)(2,1)}, bf16[1,160,384]{2,1,0:T(8,128)(2,1)S(1)}, u32[]{:S(2)}, u32[]{:S(2)}) %collective-permute-start.16) | collective-permute-done | bytes 122912 | tf_op jit(solution)/shard_map/projection_grad/ppermute | solution.py:484
  295.2 1.7 collective-permute-start.20
  296.9 1.4 collective-permute-start.22
  298.9 2.8 collective-permute-done.20.refs_4_
  301.7 2.7 collective-permute-done.22.refs_6_
  304.9 1.0 collective-permute-done.26.refs_10_
  307.5 1.6 collective-permute-start.23
  309.1 1.0 collective-permute-done.19.refs_3_
  310.1 16.8 %collective-permute-done.21.refs_5_ = bf16[3,160,384]{2,1,0:T(8,128)(2,1)} collective-permute-done((bf16[3,160,384]{2,1,0:T(8,128)(2,1)S(1)}, bf16[3,160,384]{2,1,0:T(8,128)(2,1)}, u32[]{:S(2)}, u32[]{:S(2)}) %collective-permute-start.21) | collective-permute-done | bytes 368672 | tf_op jit(solution)/shard_map/projection_grad/ppermute | solution.py:495
  328.9 2.2 output.1
  331.1 104.6 %all-reduce.5.cloned.1.call-done = bf16[896,768]{1,0:T(8,128)(2,1)} async-done(((bf16[896,768]{1,0:T(8,128)(2,1)}), bf16[896,768]{1,0:T(8,128)(2,1)}) %all-reduce.5.cloned.1.call-update) | async-done | bytes 1376272 | tf_op jit(solution)/shard_map/output_projection_grad/psum | solution.py:725
  435.7 1.6 convert_element_type.39
  437.4 1.6 slice.29
  440.2 8.1 %assemble.1 = (f32[768,2304]{1,0:T(8,128)}, f32[1,768]{1,0:T(1,128)}, f32[32,12]{1,0:T(8,128)}) custom-call(s32[96]{0:T(128)} %stack.94.sc, bf16[1,160,384]{2,1,0:T(8,128)(2,1)} %maximum_maximum_fusion.refs_0_, bf16[3,160,384]{2,1,0:T(8,128)(2,1)} %copy-done.8, bf16[1,160,384]{2,1,0:T(8,128)(2,1)} %collective-permute-done.18.refs_2_, ...), custom_call_target="tpu_custom_call" | custom-call | flops 1048576 | bytes 1048576 | tf_op jit(solution)/shard_map/projection_grad/assemble/pallas_call | solution.py:706
  448.4 1.4 copy.46
  449.8 1.3 reduce.1
  451.0 0.9 copy-done.3
  451.9 4.4 token_grads.1
  456.3 1.4 copy-done.4
  457.7 6.8 %fill.1 = (f32[768,3072]{1,0:T(8,128)}, f32[3072,768]{1,0:T(8,128)}) custom-call(s32[2]{0:T(128)} %pad_add_fusion.1.sc, bf16[768,1536]{1,0:T(8,128)(2,1)} %copy-done.4, bf16[1536,768]{1,0:T(8,128)(2,1)} %collective-permute-done.47.down_low, f32[768,3072]{1,0:T(8,128)} %get-tuple-element.64.up_full, ...), custom_call_target="tpu_custom_call", output_to_operand_aliasing={{0}: (3, {}), {1}: (4, {})} | custom-call | tf_op jit(solution)/shard_map/expert_weight_grads/fill/pallas_call | solution.py:780
  (178 shorter events, 22.0 us)
Async XLA Ops:
  7.2 11.2 %collective-permute-start = (bf16[128,768]{1,0:T(8,128)(2,1)}, bf16[128,768]{1,0:T(8,128)(2,1)S(1)}, u32[]{:S(2)}, u32[]{:S(2)}) collective-permute-start(bf16[128,768]{1,0:T(8,128)(2,1)} %bitcast.71), channel_id=1, source_target_pairs={{0,1},{1,2},{2,3},{3,0},{4,5},{5,6},{6,7},{7,4},{8,9},{9,10},{10,1... | collective-permute-start | bytes 589832 | tf_op jit(solution)/shard_map/gather_tokens/ppermute | solution.py:484
  10.3 15.7 %collective-permute-start.1 = (bf16[128,768]{1,0:T(8,128)(2,1)}, bf16[128,768]{1,0:T(8,128)(2,1)S(1)}, u32[]{:S(2)}, u32[]{:S(2)}) collective-permute-start(bf16[128,768]{1,0:T(8,128)(2,1)} %bitcast.72), channel_id=1, source_target_pairs={{0,2},{1,3},{2,0},{3,1},{4,6},{5,7},{6,4},{7,5},{8,10},{9,11},{10,... | collective-permute-start | bytes 589832 | tf_op jit(solution)/shard_map/gather_tokens/ppermute | solution.py:484
  12.9 14.6 %collective-permute-start.2 = (bf16[128,768]{1,0:T(8,128)(2,1)}, bf16[128,768]{1,0:T(8,128)(2,1)S(1)}, u32[]{:S(2)}, u32[]{:S(2)}) collective-permute-start(bf16[128,768]{1,0:T(8,128)(2,1)} %bitcast.73), channel_id=1, source_target_pairs={{0,3},{1,0},{2,1},{3,2},{4,7},{5,4},{6,5},{7,6},{8,11},{9,8},{10,9... | collective-permute-start | bytes 589832 | tf_op jit(solution)/shard_map/gather_tokens/ppermute | solution.py:484
  14.2 13.8 %collective-permute-start.3 = (bf16[128,768]{1,0:T(8,128)(2,1)}, bf16[128,768]{1,0:T(8,128)(2,1)S(1)}, u32[]{:S(2)}, u32[]{:S(2)}) collective-permute-start(bf16[128,768]{1,0:T(8,128)(2,1)} %bitcast.74), channel_id=1, source_target_pairs={{0,8},{4,12},{8,0},{12,4},{16,24},{20,28},{24,16},{28,20},{1,9},{5... | collective-permute-start | bytes 589832 | tf_op jit(solution)/shard_map/gather_tokens/ppermute | solution.py:495
  15.7 12.3 %collective-permute-start.7 = (bf16[128,768]{1,0:T(8,128)(2,1)}, bf16[128,768]{1,0:T(8,128)(2,1)S(1)}, u32[]{:S(2)}, u32[]{:S(2)}) collective-permute-start(bf16[128,768]{1,0:T(8,128)(2,1)} %bitcast.75), channel_id=1, source_target_pairs={{0,4},{4,0},{8,12},{12,8},{1,5},{5,1},{9,13},{13,9},{2,6},{6,2},{1... | collective-permute-start | bytes 589832 | tf_op jit(solution)/shard_map/gather_tokens/ppermute | solution.py:487
  18.4 10.8 %collective-permute-start.4 = (bf16[128,768]{1,0:T(8,128)(2,1)S(1)}, bf16[128,768]{1,0:T(8,128)(2,1)S(1)}, u32[]{:S(2)}, u32[]{:S(2)}) collective-permute-start(bf16[128,768]{1,0:T(8,128)(2,1)S(1)} %collective-permute-done.refs_1_), channel_id=1, source_target_pairs={{0,8},{4,12},{8,0},{12,4},{16,24},{20,28},{24,16},{28,20},{1,9},{5... | collective-permute-start | bytes 589832 | tf_op jit(solution)/shard_map/gather_tokens/ppermute | solution.py:495
  26.0 7.8 %collective-permute-start.5 = (bf16[128,768]{1,0:T(8,128)(2,1)S(1)}, bf16[128,768]{1,0:T(8,128)(2,1)S(1)}, u32[]{:S(2)}, u32[]{:S(2)}) collective-permute-start(bf16[128,768]{1,0:T(8,128)(2,1)S(1)} %collective-permute-done.1.refs_2_), channel_id=1, source_target_pairs={{0,8},{4,12},{8,0},{12,4},{16,24},{20,28},{24,16},{28,20},{1,9},{5... | collective-permute-start | bytes 589832 | tf_op jit(solution)/shard_map/gather_tokens/ppermute | solution.py:495
  27.4 9.5 %collective-permute-start.6 = (bf16[128,768]{1,0:T(8,128)(2,1)S(1)}, bf16[128,768]{1,0:T(8,128)(2,1)S(1)}, u32[]{:S(2)}, u32[]{:S(2)}) collective-permute-start(bf16[128,768]{1,0:T(8,128)(2,1)S(1)} %collective-permute-done.2.refs_3_), channel_id=1, source_target_pairs={{0,8},{4,12},{8,0},{12,4},{16,24},{20,28},{24,16},{28,20},{1,9},{5... | collective-permute-start | bytes 589832 | tf_op jit(solution)/shard_map/gather_tokens/ppermute | solution.py:495
  28.0 8.9 %collective-permute-start.10 = (bf16[128,768]{1,0:T(8,128)(2,1)S(1)}, bf16[128,768]{1,0:T(8,128)(2,1)S(1)}, u32[]{:S(2)}, u32[]{:S(2)}) collective-permute-start(bf16[128,768]{1,0:T(8,128)(2,1)S(1)} %collective-permute-done.2.refs_3_), channel_id=1, source_target_pairs={{0,4},{4,0},{8,12},{12,8},{1,5},{5,1},{9,13},{13,9},{2,6},{6,2},{1... | collective-permute-start | bytes 589832 | tf_op jit(solution)/shard_map/gather_tokens/ppermute | solution.py:487
  28.0 9.4 %collective-permute-start.8 = (bf16[128,768]{1,0:T(8,128)(2,1)S(1)}, bf16[128,768]{1,0:T(8,128)(2,1)S(1)}, u32[]{:S(2)}, u32[]{:S(2)}) collective-permute-start(bf16[128,768]{1,0:T(8,128)(2,1)S(1)} %collective-permute-done.refs_1_), channel_id=1, source_target_pairs={{0,4},{4,0},{8,12},{12,8},{1,5},{5,1},{9,13},{13,9},{2,6},{6,2},{1... | collective-permute-start | bytes 589832 | tf_op jit(solution)/shard_map/gather_tokens/ppermute | solution.py:487
  29.2 12.6 %collective-permute-start.9 = (bf16[128,768]{1,0:T(8,128)(2,1)S(1)}, bf16[128,768]{1,0:T(8,128)(2,1)S(1)}, u32[]{:S(2)}, u32[]{:S(2)}) collective-permute-start(bf16[128,768]{1,0:T(8,128)(2,1)S(1)} %collective-permute-done.1.refs_2_), channel_id=1, source_target_pairs={{0,4},{4,0},{8,12},{12,8},{1,5},{5,1},{9,13},{13,9},{2,6},{6,2},{1... | collective-permute-start | bytes 589832 | tf_op jit(solution)/shard_map/gather_tokens/ppermute | solution.py:487
  33.7 8.0 %collective-permute-start.11 = (bf16[128,768]{1,0:T(8,128)(2,1)S(1)}, bf16[128,768]{1,0:T(8,128)(2,1)S(1)}, u32[]{:S(2)}, u32[]{:S(2)}) collective-permute-start(bf16[128,768]{1,0:T(8,128)(2,1)S(1)} %collective-permute-done.3.refs_4_), channel_id=1, source_target_pairs={{0,4},{4,0},{8,12},{12,8},{1,5},{5,1},{9,13},{13,9},{2,6},{6,2},{1... | collective-permute-start | bytes 589832 | tf_op jit(solution)/shard_map/gather_tokens/ppermute | solution.py:487
  36.9 4.9 %collective-permute-start.12 = (bf16[128,768]{1,0:T(8,128)(2,1)S(1)}, bf16[128,768]{1,0:T(8,128)(2,1)S(1)}, u32[]{:S(2)}, u32[]{:S(2)}) collective-permute-start(bf16[128,768]{1,0:T(8,128)(2,1)S(1)} %collective-permute-done.4.refs_5_), channel_id=1, source_target_pairs={{0,4},{4,0},{8,12},{12,8},{1,5},{5,1},{9,13},{13,9},{2,6},{6,2},{1... | collective-permute-start | bytes 589832 | tf_op jit(solution)/shard_map/gather_tokens/ppermute | solution.py:487
  36.9 4.9 %collective-permute-start.13 = (bf16[128,768]{1,0:T(8,128)(2,1)S(1)}, bf16[128,768]{1,0:T(8,128)(2,1)}, u32[]{:S(2)}, u32[]{:S(2)}) collective-permute-start(bf16[128,768]{1,0:T(8,128)(2,1)S(1)} %collective-permute-done.5.refs_6_), channel_id=1, source_target_pairs={{0,4},{4,0},{8,12},{12,8},{1,5},{5,1},{9,13},{13,9},{2,6},{6,2},{1... | collective-permute-start | bytes 589832 | tf_op jit(solution)/shard_map/gather_tokens/ppermute | solution.py:487
  37.4 4.4 collective-permute-start.14
  56.7 39.8 %copy-start.19 = (f32[768,4]{0,1:T(4,128)S(1)}, f32[768,4]{0,1:T(4,128)}, u32[]{:S(2)}) copy-start(f32[768,4]{0,1:T(4,128)} %param.23) | copy-start | bytes 36868
  56.8 17.2 %all-to-all-start = ((bf16[16,64,128]{2,1,0:T(8,128)(2,1)}), bf16[16,64,128]{2,1,0:T(8,128)(2,1)S(1)}, u32[]{:S(2)}, u32[]{:S(2)}) async-start(bf16[16,64,128]{2,1,0:T(8,128)(2,1)} %get-tuple-element.39.refs_5_), calls=%async_computation | async-start | bytes 524288 | tf_op jit(solution)/shard_map/attention/all_to_all | solution.py:572
  73.9 19.1 %all-to-all-start.2 = ((bf16[4,80,896]{2,1,0:T(8,128)(2,1)}), bf16[4,80,896]{2,1,0:T(8,128)(2,1)S(1)}, u32[]{:S(2)}, u32[]{:S(2)}) async-start(bf16[4,80,896]{2,1,0:T(8,128)(2,1)} %bitcast.87), calls=%async_computation.2 | async-start | bytes 1146880 | tf_op jit(solution)/shard_map/routing/all_to_all | solution.py:526
  93.1 16.7 %all-to-all-start.1 = ((bf16[4,80,768]{2,1,0:T(8,128)(2,1)}), bf16[4,80,768]{2,1,0:T(8,128)(2,1)S(1)}, u32[]{:S(2)}, u32[]{:S(2)}) async-start(bf16[4,80,768]{2,1,0:T(8,128)(2,1)} %bitcast.96), calls=%async_computation.1 | async-start | bytes 983040 | tf_op jit(solution)/shard_map/middle/all_to_all | solution.py:526
  123.6 44.8 %copy-start.20 = (s32[2048]{0:T(1024)S(1)}, s32[2048]{0:T(1024)}, u32[]{:S(2)}) copy-start(s32[2048]{0:T(1024)} %param.16) | copy-start | bytes 24580
  123.7 31.6 %all-to-all-start.4 = ((bf16[4,80,768]{2,1,0:T(8,128)(2,1)}), bf16[4,80,768]{2,1,0:T(8,128)(2,1)S(1)}, u32[]{:S(2)}, u32[]{:S(2)}) async-start(bf16[4,80,768]{2,1,0:T(8,128)(2,1)} %bitcast.95), calls=%async_computation.4 | async-start | bytes 983040 | tf_op jit(solution)/shard_map/experts/all_to_all | solution.py:526
  127.5 16.2 %collective-permute-start.39 = (bf16[320,896]{1,0:T(8,128)(2,1)}, bf16[320,896]{1,0:T(8,128)(2,1)S(1)}, u32[]{:S(2)}, u32[]{:S(2)}) collective-permute-start(bf16[320,896]{1,0:T(8,128)(2,1)} %bitcast.82), channel_id=1, source_target_pairs={{0,8},{4,12},{8,0},{12,4},{16,24},{20,28},{24,16},{28,20},{1,9},{5... | collective-permute-start | bytes 1720328 | tf_op jit(solution)/shard_map/expert_weight_grads/ppermute | solution.py:495
  129.1 26.1 %collective-permute-start.40 = (bf16[320,896]{1,0:T(8,128)(2,1)}, bf16[320,896]{1,0:T(8,128)(2,1)S(1)}, u32[]{:S(2)}, u32[]{:S(2)}) collective-permute-start(bf16[320,896]{1,0:T(8,128)(2,1)} %bitcast.83), channel_id=1, source_target_pairs={{0,16},{4,20},{8,24},{12,28},{16,0},{20,4},{24,8},{28,12},{1,17},{... | collective-permute-start | bytes 1720328 | tf_op jit(solution)/shard_map/expert_weight_grads/ppermute | solution.py:495
  130.6 29.6 %collective-permute-start.41 = (bf16[320,896]{1,0:T(8,128)(2,1)}, bf16[320,896]{1,0:T(8,128)(2,1)S(1)}, u32[]{:S(2)}, u32[]{:S(2)}) collective-permute-start(bf16[320,896]{1,0:T(8,128)(2,1)} %bitcast.84), channel_id=1, source_target_pairs={{0,24},{4,28},{8,16},{12,20},{16,8},{20,12},{24,0},{28,4},{1,25},{... | collective-permute-start | bytes 1720328 | tf_op jit(solution)/shard_map/expert_weight_grads/ppermute | solution.py:495
  131.0 31.2 %collective-permute-start.42 = (bf16[320,896]{1,0:T(8,128)(2,1)}, bf16[320,896]{1,0:T(8,128)(2,1)S(1)}, u32[]{:S(2)}, u32[]{:S(2)}) collective-permute-start(bf16[320,896]{1,0:T(8,128)(2,1)} %bitcast.85), channel_id=1, source_target_pairs={{0,4},{4,0},{8,12},{12,8},{1,5},{5,1},{9,13},{13,9},{2,6},{6,2},{1... | collective-permute-start | bytes 1720328 | tf_op jit(solution)/shard_map/expert_weight_grads/ppermute | solution.py:487
  143.6 58.7 %copy-start.24 = (bf16[320,896]{1,0:T(8,128)(2,1)}, bf16[320,896]{1,0:T(8,128)(2,1)S(1)}, u32[]{:S(2)}) copy-start(bf16[320,896]{1,0:T(8,128)(2,1)S(1)} %collective-permute-done.39.refs_9_) | copy-start | bytes 1720324
  143.6 26.0 %collective-permute-start.43 = (bf16[320,896]{1,0:T(8,128)(2,1)S(1)}, bf16[320,896]{1,0:T(8,128)(2,1)}, u32[]{:S(2)}, u32[]{:S(2)}) collective-permute-start(bf16[320,896]{1,0:T(8,128)(2,1)S(1)} %collective-permute-done.39.refs_9_), channel_id=1, source_target_pairs={{0,4},{4,0},{8,12},{12,8},{1,5},{5,1},{9,13},{13,9},{2,6},{6,2},{1... | collective-permute-start | bytes 1720328 | tf_op jit(solution)/shard_map/expert_weight_grads/ppermute | solution.py:487
  155.3 47.0 %copy-start.25 = (bf16[320,896]{1,0:T(8,128)(2,1)}, bf16[320,896]{1,0:T(8,128)(2,1)S(1)}, u32[]{:S(2)}) copy-start(bf16[320,896]{1,0:T(8,128)(2,1)S(1)} %collective-permute-done.40.refs_10_) | copy-start | bytes 1720324
  155.3 14.8 %collective-permute-start.44 = (bf16[320,896]{1,0:T(8,128)(2,1)S(1)}, bf16[320,896]{1,0:T(8,128)(2,1)}, u32[]{:S(2)}, u32[]{:S(2)}) collective-permute-start(bf16[320,896]{1,0:T(8,128)(2,1)S(1)} %collective-permute-done.40.refs_10_), channel_id=1, source_target_pairs={{0,4},{4,0},{8,12},{12,8},{1,5},{5,1},{9,13},{13,9},{2,6},{6,2},{1... | collective-permute-start | bytes 1720328 | tf_op jit(solution)/shard_map/expert_weight_grads/ppermute | solution.py:487
  155.3 14.9 %collective-permute-start.32 = (bf16[320,768]{1,0:T(8,128)(2,1)}, bf16[320,768]{1,0:T(8,128)(2,1)}, u32[]{:S(2)}, u32[]{:S(2)}) collective-permute-start(bf16[320,768]{1,0:T(8,128)(2,1)} %bitcast.90), channel_id=1, source_target_pairs={{0,8},{4,12},{8,0},{12,4},{16,24},{20,28},{24,16},{28,20},{1,9},{5... | collective-permute-start | bytes 1474568 | tf_op jit(solution)/shard_map/expert_weight_grads/ppermute | solution.py:495
  160.2 42.1 %copy-start.26 = (bf16[320,896]{1,0:T(8,128)(2,1)}, bf16[320,896]{1,0:T(8,128)(2,1)S(1)}, u32[]{:S(2)}) copy-start(bf16[320,896]{1,0:T(8,128)(2,1)S(1)} %collective-permute-done.41.refs_11_) | copy-start | bytes 1720324
  160.2 24.3 %collective-permute-start.33 = (bf16[320,768]{1,0:T(8,128)(2,1)S(1)}, bf16[320,768]{1,0:T(8,128)(2,1)}, u32[]{:S(2)}, u32[]{:S(2)}) collective-permute-start(bf16[320,768]{1,0:T(8,128)(2,1)S(1)} %bitcast.92), channel_id=1, source_target_pairs={{0,16},{4,20},{8,24},{12,28},{16,0},{20,4},{24,8},{28,12},{1,17},{... | collective-permute-start | bytes 1474568 | tf_op jit(solution)/shard_map/expert_weight_grads/ppermute | solution.py:495
  162.2 40.1 %copy-start.27 = (bf16[320,896]{1,0:T(8,128)(2,1)}, bf16[320,896]{1,0:T(8,128)(2,1)S(1)}, u32[]{:S(2)}) copy-start(bf16[320,896]{1,0:T(8,128)(2,1)S(1)} %collective-permute-done.42.refs_12_) | copy-start | bytes 1720324
  162.2 22.3 %collective-permute-start.34 = (bf16[320,768]{1,0:T(8,128)(2,1)S(1)}, bf16[320,768]{1,0:T(8,128)(2,1)}, u32[]{:S(2)}, u32[]{:S(2)}) collective-permute-start(bf16[320,768]{1,0:T(8,128)(2,1)S(1)} %bitcast.93), channel_id=1, source_target_pairs={{0,24},{4,28},{8,16},{12,20},{16,8},{20,12},{24,0},{28,4},{1,25},{... | collective-permute-start | bytes 1474568 | tf_op jit(solution)/shard_map/expert_weight_grads/ppermute | solution.py:495
  163.7 21.3 %all-to-all-start.5 = ((bf16[16,64,128]{2,1,0:T(8,128)(2,1)}), bf16[16,64,128]{2,1,0:T(8,128)(2,1)S(1)}, u32[]{:S(2)}, u32[]{:S(2)}) async-start(bf16[16,64,128]{2,1,0:T(8,128)(2,1)} %get-tuple-element.52), calls=%async_computation.5 | async-start | bytes 524288 | tf_op jit(solution)/shard_map/middle_back/all_to_all | solution.py:637
  169.6 36.7 %collective-permute-start.45 = (bf16[320,896]{1,0:T(8,128)(2,1)S(1)}, bf16[320,896]{1,0:T(8,128)(2,1)}, u32[]{:S(2)}, u32[]{:S(2)}) collective-permute-start(bf16[320,896]{1,0:T(8,128)(2,1)S(1)} %collective-permute-done.41.refs_11_), channel_id=1, source_target_pairs={{0,4},{4,0},{8,12},{12,8},{1,5},{5,1},{9,13},{13,9},{2,6},{6,2},{1... | collective-permute-start | bytes 1720328 | tf_op jit(solution)/shard_map/expert_weight_grads/ppermute | solution.py:487
  170.1 36.3 %collective-permute-start.35 = (bf16[320,768]{1,0:T(8,128)(2,1)S(1)}, bf16[320,768]{1,0:T(8,128)(2,1)}, u32[]{:S(2)}, u32[]{:S(2)}) collective-permute-start(bf16[320,768]{1,0:T(8,128)(2,1)S(1)} %bitcast.94), channel_id=1, source_target_pairs={{0,4},{4,0},{8,12},{12,8},{1,5},{5,1},{9,13},{13,9},{2,6},{6,2},{1... | collective-permute-start | bytes 1474568 | tf_op jit(solution)/shard_map/expert_weight_grads/ppermute | solution.py:487
  170.2 36.2 %collective-permute-start.36 = (bf16[320,768]{1,0:T(8,128)(2,1)}, bf16[320,768]{1,0:T(8,128)(2,1)}, u32[]{:S(2)}, u32[]{:S(2)}) collective-permute-start(bf16[320,768]{1,0:T(8,128)(2,1)} %collective-permute-done.32.refs_1_), channel_id=1, source_target_pairs={{0,4},{4,0},{8,12},{12,8},{1,5},{5,1},{9,13},{13,9},{2,6},{6,2},{1... | collective-permute-start | bytes 1474568 | tf_op jit(solution)/shard_map/expert_weight_grads/ppermute | solution.py:487
  184.5 21.8 %collective-permute-start.37 = (bf16[320,768]{1,0:T(8,128)(2,1)}, bf16[320,768]{1,0:T(8,128)(2,1)}, u32[]{:S(2)}, u32[]{:S(2)}) collective-permute-start(bf16[320,768]{1,0:T(8,128)(2,1)} %collective-permute-done.33.refs_2_), channel_id=1, source_target_pairs={{0,4},{4,0},{8,12},{12,8},{1,5},{5,1},{9,13},{13,9},{2,6},{6,2},{1... | collective-permute-start | bytes 1474568 | tf_op jit(solution)/shard_map/expert_weight_grads/ppermute | solution.py:487
  184.5 21.8 %collective-permute-start.38 = (bf16[320,768]{1,0:T(8,128)(2,1)}, bf16[320,768]{1,0:T(8,128)(2,1)}, u32[]{:S(2)}, u32[]{:S(2)}) collective-permute-start(bf16[320,768]{1,0:T(8,128)(2,1)} %collective-permute-done.34.refs_3_), channel_id=1, source_target_pairs={{0,4},{4,0},{8,12},{12,8},{1,5},{5,1},{9,13},{13,9},{2,6},{6,2},{1... | collective-permute-start | bytes 1474568 | tf_op jit(solution)/shard_map/expert_weight_grads/ppermute | solution.py:487
  202.3 40.3 %all-to-all-start.7 = ((bf16[8,64,384]{2,1,0:T(8,128)(2,1)}), bf16[8,64,384]{2,1,0:T(8,128)(2,1)S(1)}, u32[]{:S(2)}, u32[]{:S(2)}) async-start(bf16[8,64,384]{2,1,0:T(8,128)(2,1)} %get-tuple-element.57), calls=%async_computation.7 | async-start | bytes 786432 | tf_op jit(solution)/shard_map/attention_back/all_to_all | solution.py:668
  242.0 214.3 %collective-permute-start.46 = (bf16[768,1536]{1,0:T(8,128)(2,1)}, bf16[768,1536]{1,0:T(8,128)(2,1)S(1)}, u32[]{:S(2)}, u32[]{:S(2)}) collective-permute-start(bf16[768,1536]{1,0:T(8,128)(2,1)} %get-tuple-element.62), channel_id=1, source_target_pairs={{0,4},{4,0},{8,12},{12,8},{1,5},{5,1},{9,13},{13,9},{2,6},{6,2},{1... | collective-permute-start | bytes 7077896 | tf_op jit(solution)/shard_map/expert_weight_grads/ppermute | solution.py:487
  242.6 213.8 %collective-permute-start.47 = (bf16[1536,768]{1,0:T(8,128)(2,1)}, bf16[1536,768]{1,0:T(8,128)(2,1)}, u32[]{:S(2)}, u32[]{:S(2)}) collective-permute-start(bf16[1536,768]{1,0:T(8,128)(2,1)} %get-tuple-element.63), channel_id=1, source_target_pairs={{0,4},{4,0},{8,12},{12,8},{1,5},{5,1},{9,13},{13,9},{2,6},{6,2},{1... | collective-permute-start | bytes 7077896 | tf_op jit(solution)/shard_map/expert_weight_grads/ppermute | solution.py:487
  242.6 21.6 %all-to-all-start.3 = ((bf16[4,80,768]{2,1,0:T(8,128)(2,1)}), bf16[4,80,768]{2,1,0:T(8,128)(2,1)S(1)}, u32[]{:S(2)}, u32[]{:S(2)}) async-start(bf16[4,80,768]{2,1,0:T(8,128)(2,1)} %bitcast.88), calls=%async_computation.3 | async-start | bytes 983040 | tf_op jit(solution)/shard_map/experts/all_to_all | solution.py:526
  248.1 24.8 %collective-permute-start.15 = (bf16[1,160,384]{2,1,0:T(8,128)(2,1)}, bf16[1,160,384]{2,1,0:T(8,128)(2,1)S(1)}, u32[]{:S(2)}, u32[]{:S(2)}) collective-permute-start(bf16[1,160,384]{2,1,0:T(8,128)(2,1)} %maximum_maximum_fusion.refs_0_), channel_id=1, source_target_pairs={{0,1},{1,2},{2,3},{3,0},{4,5},{5,6},{6,7},{7,4},{8,9},{9,10},{10,1... | collective-permute-start | bytes 368648 | tf_op jit(solution)/shard_map/projection_grad/ppermute | solution.py:484
  265.0 186.1 %all-to-all-start.6 = ((bf16[16,192,128]{2,1,0:T(8,128)(2,1)}), bf16[16,192,128]{2,1,0:T(8,128)(2,1)S(1)}, u32[]{:S(2)}, u32[]{:S(2)}) async-start(bf16[16,192,128]{2,1,0:T(8,128)(2,1)} %get-tuple-element.55), calls=%async_computation.6 | async-start | bytes 1572864 | tf_op jit(solution)/shard_map/attention_back/all_to_all | solution.py:669
  268.6 167.1 %all-reduce.5.cloned.1.call-start = ((), (), s32[]{:S(2)}) async-start(), calls=%async_computation.8 | async-start | bytes 2752512 | tf_op jit(solution)/shard_map/output_projection_grad/psum | solution.py:725
  268.6 26.5 %collective-permute-start.16 = (bf16[1,160,384]{2,1,0:T(8,128)(2,1)}, bf16[1,160,384]{2,1,0:T(8,128)(2,1)S(1)}, u32[]{:S(2)}, u32[]{:S(2)}) collective-permute-start(bf16[1,160,384]{2,1,0:T(8,128)(2,1)} %maximum_maximum_fusion.refs_0_), channel_id=1, source_target_pairs={{0,2},{1,3},{2,0},{3,1},{4,6},{5,7},{6,4},{7,5},{8,10},{9,11},{10,... | collective-permute-start | bytes 368648 | tf_op jit(solution)/shard_map/projection_grad/ppermute | solution.py:484
  271.4 25.4 %collective-permute-start.17 = (bf16[1,160,384]{2,1,0:T(8,128)(2,1)}, bf16[1,160,384]{2,1,0:T(8,128)(2,1)S(1)}, u32[]{:S(2)}, u32[]{:S(2)}) collective-permute-start(bf16[1,160,384]{2,1,0:T(8,128)(2,1)} %maximum_maximum_fusion.refs_0_), channel_id=1, source_target_pairs={{0,3},{1,0},{2,1},{3,2},{4,7},{5,4},{6,5},{7,6},{8,11},{9,8},{10,9... | collective-permute-start | bytes 368648 | tf_op jit(solution)/shard_map/projection_grad/ppermute | solution.py:484
  273.5 24.7 %collective-permute-start.18 = (bf16[1,160,384]{2,1,0:T(8,128)(2,1)}, bf16[1,160,384]{2,1,0:T(8,128)(2,1)}, u32[]{:S(2)}, u32[]{:S(2)}) collective-permute-start(bf16[1,160,384]{2,1,0:T(8,128)(2,1)} %maximum_maximum_fusion.refs_0_), channel_id=1, source_target_pairs={{0,8},{4,12},{8,0},{12,4},{16,24},{20,28},{24,16},{28,20},{1,9},{5... | collective-permute-start | bytes 368648 | tf_op jit(solution)/shard_map/projection_grad/ppermute | solution.py:495
  295.2 6.5 %collective-permute-start.20 = (bf16[1,160,384]{2,1,0:T(8,128)(2,1)}, bf16[1,160,384]{2,1,0:T(8,128)(2,1)}, u32[]{:S(2)}, u32[]{:S(2)}) collective-permute-start(bf16[1,160,384]{2,1,0:T(8,128)(2,1)} %maximum_maximum_fusion.refs_0_), channel_id=1, source_target_pairs={{0,16},{4,20},{8,24},{12,28},{16,0},{20,4},{24,8},{28,12},{1,17},{... | collective-permute-start | bytes 368648 | tf_op jit(solution)/shard_map/projection_grad/ppermute | solution.py:495
  296.9 7.5 %collective-permute-start.22 = (bf16[1,160,384]{2,1,0:T(8,128)(2,1)}, bf16[1,160,384]{2,1,0:T(8,128)(2,1)}, u32[]{:S(2)}, u32[]{:S(2)}) collective-permute-start(bf16[1,160,384]{2,1,0:T(8,128)(2,1)} %maximum_maximum_fusion.refs_0_), channel_id=1, source_target_pairs={{0,24},{4,28},{8,16},{12,20},{16,8},{20,12},{24,0},{28,4},{1,25},{... | collective-permute-start | bytes 368648 | tf_op jit(solution)/shard_map/projection_grad/ppermute | solution.py:495
  298.3 139.1 %copy-start.8 = (bf16[3,160,384]{2,1,0:T(8,128)(2,1)}, bf16[3,160,384]{2,1,0:T(8,128)(2,1)S(1)}, u32[]{:S(2)}) copy-start(bf16[3,160,384]{2,1,0:T(8,128)(2,1)S(1)} %constant_dynamic-update-slice_fusion.refs_1_) | copy-start | bytes 1105924
  298.3 11.8 %collective-permute-start.19 = (bf16[3,160,384]{2,1,0:T(8,128)(2,1)S(1)}, bf16[3,160,384]{2,1,0:T(8,128)(2,1)}, u32[]{:S(2)}, u32[]{:S(2)}) collective-permute-start(bf16[3,160,384]{2,1,0:T(8,128)(2,1)S(1)} %constant_dynamic-update-slice_fusion.refs_1_), channel_id=1, source_target_pairs={{0,8},{4,12},{8,0},{12,4},{16,24},{20,28},{24,16},{28,20},{1,9},{5... | collective-permute-start | bytes 1105928 | tf_op jit(solution)/shard_map/projection_grad/ppermute | solution.py:495
  301.7 2.7 collective-permute-start.24
  304.4 1.5 collective-permute-start.26
  304.4 1.7 collective-permute-start.28
  305.9 1.5 collective-permute-start.30
  306.1 20.8 %collective-permute-start.21 = (bf16[3,160,384]{2,1,0:T(8,128)(2,1)S(1)}, bf16[3,160,384]{2,1,0:T(8,128)(2,1)}, u32[]{:S(2)}, u32[]{:S(2)}) collective-permute-start(bf16[3,160,384]{2,1,0:T(8,128)(2,1)S(1)} %constant_dynamic-update-slice_fusion.refs_1_), channel_id=1, source_target_pairs={{0,16},{4,20},{8,24},{12,28},{16,0},{20,4},{24,8},{28,12},{1,17},{... | collective-permute-start | bytes 1105928 | tf_op jit(solution)/shard_map/projection_grad/ppermute | solution.py:495
  307.5 19.4 %collective-permute-start.23 = (bf16[3,160,384]{2,1,0:T(8,128)(2,1)S(1)}, bf16[3,160,384]{2,1,0:T(8,128)(2,1)}, u32[]{:S(2)}, u32[]{:S(2)}) collective-permute-start(bf16[3,160,384]{2,1,0:T(8,128)(2,1)S(1)} %constant_dynamic-update-slice_fusion.refs_1_), channel_id=1, source_target_pairs={{0,24},{4,28},{8,16},{12,20},{16,8},{20,12},{24,0},{28,4},{1,25},{... | collective-permute-start | bytes 1105928 | tf_op jit(solution)/shard_map/projection_grad/ppermute | solution.py:495
  310.1 17.3 %collective-permute-start.25 = (bf16[3,160,384]{2,1,0:T(8,128)(2,1)S(1)}, bf16[3,160,384]{2,1,0:T(8,128)(2,1)S(1)}, u32[]{:S(2)}, u32[]{:S(2)}) collective-permute-start(bf16[3,160,384]{2,1,0:T(8,128)(2,1)S(1)} %constant_dynamic-update-slice_fusion.refs_1_), channel_id=1, source_target_pairs={{0,4},{4,0},{8,12},{12,8},{1,5},{5,1},{9,13},{13,9},{2,6},{6,2},{1... | collective-permute-start | bytes 1105928 | tf_op jit(solution)/shard_map/projection_grad/ppermute | solution.py:487
  326.9 113.3 %collective-permute-start.27 = (bf16[3,160,384]{2,1,0:T(8,128)(2,1)}, bf16[3,160,384]{2,1,0:T(8,128)(2,1)}, u32[]{:S(2)}, u32[]{:S(2)}) collective-permute-start(bf16[3,160,384]{2,1,0:T(8,128)(2,1)} %collective-permute-done.19.refs_3_), channel_id=1, source_target_pairs={{0,4},{4,0},{8,12},{12,8},{1,5},{5,1},{9,13},{13,9},{2,6},{6,2},{1... | collective-permute-start | bytes 1105928 | tf_op jit(solution)/shard_map/projection_grad/ppermute | solution.py:487
  326.9 113.3 %collective-permute-start.29 = (bf16[3,160,384]{2,1,0:T(8,128)(2,1)}, bf16[3,160,384]{2,1,0:T(8,128)(2,1)}, u32[]{:S(2)}, u32[]{:S(2)}) collective-permute-start(bf16[3,160,384]{2,1,0:T(8,128)(2,1)} %collective-permute-done.21.refs_5_), channel_id=1, source_target_pairs={{0,4},{4,0},{8,12},{12,8},{1,5},{5,1},{9,13},{13,9},{2,6},{6,2},{1... | collective-permute-start | bytes 1105928 | tf_op jit(solution)/shard_map/projection_grad/ppermute | solution.py:487
  328.1 112.1 %collective-permute-start.31 = (bf16[3,160,384]{2,1,0:T(8,128)(2,1)}, bf16[3,160,384]{2,1,0:T(8,128)(2,1)}, u32[]{:S(2)}, u32[]{:S(2)}) collective-permute-start(bf16[3,160,384]{2,1,0:T(8,128)(2,1)} %collective-permute-done.23.refs_7_), channel_id=1, source_target_pairs={{0,4},{4,0},{8,12},{12,8},{1,5},{5,1},{9,13},{13,9},{2,6},{6,2},{1... | collective-permute-start | bytes 1105928 | tf_op jit(solution)/shard_map/projection_grad/ppermute | solution.py:487
  (34 other events, 345.8 us)
Sparse Core Ops, SparseCore 0:
  299.0 136.6 all-reduce.4
